TPU v7x, 512 devices: a whole 4x8x8 slice. The times are simulated.
512 devices in a mesh: node: 32 (over z_lo, x, core), group: 16 (over y, z_hi).
Axes of the slice: x: 4, y: 8, z: 8 (z_hi: 2, z_lo: 4; z = z_hi * 4 + z_lo), core: 2. Of those that a mesh axis runs over, the one named last changes fastest.
Arguments:
- tokens: bfloat16 [131072, 1024], P(('node', 'group')), may hold values from -6 to 6
- grad_out: bfloat16 [131072, 1024], P(('node', 'group')), may hold values from -1.5 to 1.5
- router_gate: float32 [131072, 4], P(('node', 'group')), may hold values from 0.1 to 1
- counts: int32 [512], P(('node', 'group')), may hold values from 1 to 2
- routes: int32 [512, 2, 4], P(('node', 'group')), may hold values from 0 to 15, as said below
- partner: int32 [32], replicated, may hold values from 0 to 31, as said below
- w_gate: bfloat16 [512, 1024, 256], P(('node', 'group')), may hold values from -0.1875 to 0.1875
- w_up: bfloat16 [512, 1024, 256], P(('node', 'group')), may hold values from -0.1875 to 0.1875
- w_down: bfloat16 [512, 256, 1024], P(('node', 'group')), may hold values from -0.375 to 0.375
Outputs:
- grad_tokens: bfloat16 [131072, 1024], P(('node', 'group'))
- grad_gate: bfloat16 [512, 1024, 256], P(('node', 'group'))
- grad_up: bfloat16 [512, 1024, 256], P(('node', 'group'))
- grad_down: bfloat16 [512, 256, 1024], P(('node', 'group'))
Inputs may be any that keep to these rules, and one draw needn't show every extreme that they name: `routes`: the 8 entries of one device name different devices of its group; every device of a group is named; in every node group one device is named by exactly 12 entries and none by more. partner pairs the nodes: partner[partner[n]] = n and partner[n] != n.
All inputs are finite; a program needn't handle non-finite values.
Results may differ from a plain program's by a relative error of at most 0.015.
Values may be sent and summed in bfloat16 or wider, within the bound.
A program may use at most 128 MiB of HBM per device.

v0:
```python
import math

import jax
import jax.numpy as jnp
from jax import lax
from jax.sharding import PartitionSpec as P


def side_by_side(arrays, axis, split_dim, concat_dim, along):
    widths = [math.prod(a.shape[along:]) for a in arrays]
    both = jnp.concatenate(
        [a.reshape(*a.shape[:along], w) for a, w in zip(arrays, widths)], axis=along
    )
    result = lax.all_to_all(both, axis, split_axis=split_dim, concat_axis=concat_dim, tiled=True)
    tiles = jnp.split(result, [sum(widths[:k]) for k in range(1, len(widths))], axis=along)
    return tuple(
        (b.reshape(*result.shape[:along], *a.shape[along:]) for a, b in zip(arrays, tiles))
    )


def sent_to_all(x, axis):
    copies = jnp.broadcast_to(x, (lax.axis_size(axis), *x.shape))
    return lax.all_to_all(copies, axis, split_axis=0, concat_axis=0, tiled=True)


def in_order(tiles, dim):
    tiles = jnp.moveaxis(tiles, 0, dim)
    dims = tiles.shape
    return tiles.reshape(*dims[:dim], dims[dim] * dims[dim + 1], *dims[dim + 2 :])


def gathered_copies(x, axis, dim):
    tiles = sent_to_all(x, axis)
    return in_order(tiles, dim)


def against(left, right):
    return lax.dot_general(
        left, right, (((1,), (1,)), ((), ())), preferred_element_type=jnp.float32
    )


def across(left, right):
    return lax.dot_general(
        left, right, (((0,), (0,)), ((), ())), preferred_element_type=jnp.float32
    )


def forward_pass(rows, w_gate, w_up):
    gate_pre = jnp.dot(rows, w_gate, preferred_element_type=jnp.float32)
    up_pre = jnp.dot(rows, w_up, preferred_element_type=jnp.float32)
    sigmoid = jax.nn.sigmoid(gate_pre)
    swish = gate_pre * sigmoid
    hidden = (swish * up_pre).astype(jnp.bfloat16)
    return (gate_pre, up_pre, sigmoid, swish, hidden)


def relocate(w_gate, w_up, w_down, partner):
    nodes = lax.axis_size("node")
    depth, width = (w_gate.shape[1], w_gate.shape[2])
    gate_parts = w_gate.reshape(nodes, depth // nodes, width)
    up_parts = w_up.reshape(nodes, depth // nodes, width)
    down_parts = w_down.reshape(nodes, width // nodes, depth)
    mixed = (
        lax.all_to_all(gate_parts, "node", split_axis=0, concat_axis=0, tiled=True),
        lax.all_to_all(up_parts, "node", split_axis=0, concat_axis=0, tiled=True),
        lax.all_to_all(down_parts, "node", split_axis=0, concat_axis=0, tiled=True),
    )
    gate_pick = jnp.take(mixed[0], partner, axis=0)
    up_pick = jnp.take(mixed[1], partner, axis=0)
    down_pick = jnp.take(mixed[2], partner, axis=0)
    placed = side_by_side((gate_pick, up_pick, down_pick), "node", 0, 0, 1)
    return (
        placed[0].reshape(depth, width),
        placed[1].reshape(depth, width),
        placed[2].reshape(width, depth),
    )


def on_device(tokens, grad_out, router_gate, counts, routes, partner, w_gate, w_up, w_down):
    group = lax.axis_size("group")
    slots_dev, topk = (routes.shape[1], routes.shape[2])
    spread = slots_dev * topk
    capacity = spread + spread // 2
    block = tokens.shape[0] // slots_dev
    depth = tokens.shape[1]
    shard_rows = slots_dev * block
    placed_gate, placed_up, placed_down = relocate(w_gate, w_up, w_down, partner)
    live_rows = (jnp.arange(shard_rows, dtype=jnp.int32) // block < counts[0])[:, None]
    masked_tok = jnp.where(live_rows, tokens, jnp.zeros((), jnp.bfloat16))
    masked_out = jnp.where(live_rows, grad_out, jnp.zeros((), jnp.bfloat16))
    table = gathered_copies(routes, "group", 0)
    myself = lax.axis_index("group")
    flat = table.reshape(group * spread)
    chosen = flat == myself
    index = jnp.argsort(jnp.where(chosen, 0, 1).astype(jnp.int32), stable=True)[:capacity]
    valid = chosen[index]
    sources = index // spread
    own_block = index % spread // topk
    column = index % topk
    targets = jnp.arange(group, dtype=jnp.int32)
    onehot = (routes[0][None, :, :] == targets[:, None, None]).astype(jnp.bfloat16)
    pick = ((sources[:, None] == targets[None, :]) & valid[:, None]).astype(jnp.bfloat16)
    wanted = sources * shard_rows + own_block * block
    column_hot = (jnp.arange(topk, dtype=jnp.int32)[None, :] == column[:, None]).astype(jnp.float32)
    empty = jnp.zeros((capacity, block, depth), jnp.bfloat16)
    tok_piece = lax.all_gather(masked_tok, "group", axis=0, tiled=True)
    out_piece = lax.all_gather(masked_out, "group", axis=0, tiled=True)
    gate_piece = lax.all_gather(
        router_gate.astype(jnp.bfloat16), "group", axis=0, tiled=True
    ).astype(jnp.float32)
    length = tok_piece.shape[0]
    inside = valid & (wanted >= 0) & (wanted + block <= length)
    offset = jnp.clip(wanted, 0, length - block)

    def take_one(where_at):
        return (
            lax.dynamic_slice_in_dim(tok_piece, where_at, block, 0),
            lax.dynamic_slice_in_dim(out_piece, where_at, block, 0),
            lax.dynamic_slice_in_dim(gate_piece, where_at, block, 0),
        )

    tok_sel, out_sel, gate_sel = jax.vmap(take_one)(offset)
    weight = jnp.sum(gate_sel * column_hot[:, None, :], axis=2)
    scaled_sel = (weight[:, :, None] * out_sel.astype(jnp.float32)).astype(jnp.bfloat16)
    keep = inside[:, None, None]
    got_tok = jnp.where(keep, tok_sel, empty)
    got_grad = jnp.where(keep, scaled_sel, empty)
    rows = got_tok.reshape(capacity * block, depth)
    grads = got_grad.reshape(capacity * block, depth)
    gate_pre, up_pre, sigmoid, swish, hidden = forward_pass(rows, placed_gate, placed_up)
    grad_hidden = against(grads, placed_down)
    grad_upre = (grad_hidden * swish).astype(jnp.bfloat16)
    grad_gpre = (grad_hidden * up_pre * sigmoid * (1.0 + gate_pre * (1.0 - sigmoid))).astype(
        jnp.bfloat16
    )
    grad_wg = across(rows, grad_gpre).astype(jnp.bfloat16)
    grad_wu = across(rows, grad_upre).astype(jnp.bfloat16)
    grad_wd = across(hidden, grads).astype(jnp.bfloat16)
    inputs_grad = (against(grad_gpre, placed_gate) + against(grad_upre, placed_up)).astype(
        jnp.bfloat16
    )
    slots = jnp.einsum(
        "rg,rsd->gsd",
        pick,
        inputs_grad.reshape(capacity, block, depth),
        preferred_element_type=jnp.float32,
    ).astype(jnp.bfloat16)
    returned = lax.all_to_all(slots, "group", split_axis=0, concat_axis=0, tiled=True)
    mine = jnp.einsum("gbk,gsd->bsd", onehot, returned, preferred_element_type=jnp.float32)
    mine = mine.astype(jnp.bfloat16).reshape(shard_rows, depth)
    grad_tokens = jnp.where(live_rows, mine, jnp.zeros((), jnp.bfloat16))
    width = placed_gate.shape[1]
    return (
        grad_tokens,
        grad_wg.reshape(1, depth, width),
        grad_wu.reshape(1, depth, width),
        grad_wd.reshape(1, width, depth),
    )


def solution(mesh):
    return jax.shard_map(
        on_device,
        mesh=mesh,
        in_specs=(
            P(("node", "group"), None),
            P(("node", "group"), None),
            P(("node", "group"), None),
            P(("node", "group")),
            P(("node", "group"), None, None),
            P(),
            P(("node", "group"), None, None),
            P(("node", "group"), None, None),
            P(("node", "group"), None, None),
        ),
        out_specs=(
            P(("node", "group"), None),
            P(("node", "group"), None, None),
            P(("node", "group"), None, None),
            P(("node", "group"), None, None),
        ),
        check_vma=False,
    )
```

profile of v0, /device:TPU:6, one launch (start us, length us, event | category | flops | bytes accessed | tf_op | source)
XLA Modules:
  0.0 637.3 jit_solution(11685429359600773166)
XLA Ops:
  8.0 2.3 broadcast_select_fusion.5
  11.1 27.9 %all_to_all.37 = s32[16,1,2,4]{3,2,1,0:T(2,128)S(1)} all-to-all(s32[16,1,2,4]{3,2,1,0:T(2,128)S(1)} %broadcast_in_dim.93), channel_id=1, replica_groups=mesh['node'=32,'group'=16] {'group'}, dimensions={0} | all-to-all | bytes 1024 | tf_op jit(solution)/shard_map/all_to_all | solution.py:23
  39.0 22.8 %all_to_all.38 = bf16[32,32,256]{2,1,0:T(8,128)(2,1)S(1)} all-to-all(bf16[32,32,256]{2,1,0:T(8,128)(2,1)S(1)} %bitcast.94), channel_id=1, replica_groups=mesh['node'=32,'group'=16] {'node'}, dimensions={0} | all-to-all | bytes 1048576 | tf_op jit(solution)/shard_map/all_to_all | solution.py:65
  61.8 5.8 all-to-all-start.2
  67.6 53.6 %all_gather.9 = bf16[4096,4]{0,1:T(4,128)(2,1)S(1)} all-gather(bf16[256,4]{0,1:T(4,128)(2,1)S(1)} %convert_element_type.78), channel_id=1, replica_groups=mesh['node'=32,'group'=16] {'group'}, dimensions={0}, use_global_device_ids=true | all-gather | bytes 34816 | tf_op jit(solution)/shard_map/all_gather | solution.py:109
  121.4 11.1 %all-to-all-start.3 = ((bf16[32,8,1024]{2,1,0:T(8,128)(2,1)}), bf16[32,8,1024]{2,1,0:T(8,128)(2,1)S(1)}, u32[]{:S(2)}, u32[]{:S(2)}) async-start(bf16[32,8,1024]{2,1,0:T(8,128)(2,1)} %bitcast.8), calls=%async_computation.3 | async-start | bytes 1048576 | tf_op jit(solution)/shard_map/all_to_all | solution.py:67
  132.5 2.5 sort.17
  137.7 54.0 %all-to-all-done.3 = bf16[32,8,1024]{2,1,0:T(8,128)(2,1)S(1)} async-done(((bf16[32,8,1024]{2,1,0:T(8,128)(2,1)}), bf16[32,8,1024]{2,1,0:T(8,128)(2,1)S(1)}, u32[]{:S(2)}, u32[]{:S(2)}) %all-to-all-start.3) | async-done | bytes 524320 | tf_op jit(solution)/shard_map/all_to_all | solution.py:67
  193.4 1.9 reduce
  195.3 2.1 reshape.318
  197.4 5.3 all-to-all-start.4
  202.7 15.8 %while.3 = (s32[]{:T(128)}, f32[4096,4]{0,1:T(4,128)S(1)}, s32[12,2]{0,1:T(2,128)S(1)}, f32[12,128,4]{1,2,0:T(4,128)S(1)}, s32[]{:T(128)}) while((s32[]{:T(128)}, f32[4096,4]{0,1:T(4,128)S(1)}, s32[12,2]{0,1:T(2,128)S(1)}, f32[12,128,4]{1,2,0:T(4,128)S(1)}, s32[]{:T(128)}) %tuple.54), condition=%wide.while_cond, body=%wide.while_body.sunk | while | flops 2 | bytes 4193 | solution.py:120
  218.6 21.3 %all-to-all-done.4 = bf16[32,2,12288]{2,1,0:T(2,128)(2,1)} async-done(((bf16[32,2,12288]{2,1,0:T(2,128)(2,1)}), bf16[32,2,12288]{2,1,0:T(2,128)(2,1)}, u32[]{:S(2)}, u32[]{:S(2)}) %all-to-all-start.4) | async-done | bytes 1572896 | tf_op jit(solution)/shard_map/all_to_all | solution.py:14
  240.0 8.2 %reshape.319 = bf16[32,1,24576]{2,1,0:T(2,128)(2,1)S(1)} reshape(bf16[32,2,12288]{2,1,0:T(2,128)(2,1)} %all-to-all-done.4) | data formatting | bytes 3145728
  248.2 1.7 copy.41
  253.5 27.4 %while.4 = (s32[]{:T(128)}, bf16[4096,1024]{1,0:T(8,128)(2,1)}, s32[12,2]{0,1:T(2,128)S(1)}, bf16[12,128,1024]{2,1,0:T(8,128)(2,1)S(1)}, s32[]{:T(128)}) while((s32[]{:T(128)}, bf16[4096,1024]{1,0:T(8,128)(2,1)}, s32[12,2]{0,1:T(2,128)S(1)}, bf16[12,128,1024]{2,1,0:T(8,128)(2,1)S(1)}, s32[]{:T(128)}) %tuple.67), condition=%wide.while_cond.1, body=%wide.while_body.1.sunk | while | flops 2 | bytes 524385 | solution.py:119
  263.3 1.7 bitcast_dynamic-update-slice_fusion.7
  267.8 1.7 bitcast_dynamic-update-slice_fusion.7
  272.4 1.7 bitcast_dynamic-update-slice_fusion.7
  281.0 1.7 copy-done
  282.7 136.1 %all-gather.5.cloned.1.call-done = bf16[4096,1024]{1,0:T(8,128)(2,1)} async-done(((bf16[256,1024]{1,0:T(8,128)(2,1)}), bf16[4096,1024]{1,0:T(8,128)(2,1)}) %all-gather.5.cloned.1.call-update) | async-done | bytes 8388624 | tf_op jit(solution)/shard_map/all_gather | solution.py:107
  419.1 27.4 %while.5 = (s32[]{:T(128)}, bf16[4096,1024]{1,0:T(8,128)(2,1)}, s32[12,2]{0,1:T(2,128)S(1)}, bf16[12,128,1024]{2,1,0:T(8,128)(2,1)S(1)}, s32[]{:T(128)}) while((s32[]{:T(128)}, bf16[4096,1024]{1,0:T(8,128)(2,1)}, s32[12,2]{0,1:T(2,128)S(1)}, bf16[12,128,1024]{2,1,0:T(8,128)(2,1)S(1)}, s32[]{:T(128)}) %tuple.68), condition=%wide.while_cond.2, body=%wide.while_body.2.sunk | while | flops 2 | bytes 524385 | solution.py:118
  446.5 3.4 fusion.5
  456.1 2.5 fusion.7
  458.6 4.3 copy.25
  462.9 4.8 all-to-all-start.5
  467.9 3.1 fusion.6
  471.0 1.8 fusion.14
  472.9 1.8 fusion.15
  474.7 1.9 fusion.16
  476.7 148.0 %all-to-all-done.5 = bf16[16,128,1024]{2,1,0:T(8,128)(2,1)} async-done(((bf16[16,128,1024]{2,1,0:T(8,128)(2,1)}), bf16[16,128,1024]{2,1,0:T(8,128)(2,1)}, u32[]{:S(2)}, u32[]{:S(2)}) %all-to-all-start.5) | async-done | bytes 4194336 | tf_op jit(solution)/shard_map/all_to_all | solution.py:149
  624.7 4.7 fusion.11
  (187 shorter events, 81.7 us)
Async XLA Ops:
  7.2 3.9 copy-start.10
  7.2 31.8 %copy-start.7 = (bf16[1,1024,256]{2,1,0:T(8,128)(2,1)S(1)}, bf16[1,1024,256]{2,1,0:T(8,128)(2,1)}, u32[]{:S(2)}) copy-start(bf16[1,1024,256]{2,1,0:T(8,128)(2,1)} %param.17) | copy-start | bytes 1572868
  7.2 60.4 %copy-start.9 = (f32[256,4]{0,1:T(4,128)S(1)}, f32[256,4]{0,1:T(4,128)}, u32[]{:S(2)}) copy-start(f32[256,4]{0,1:T(4,128)} %param.13) | copy-start | bytes 12292
  7.2 114.0 %copy-start.11 = (s32[32]{0:T(128)S(1)}, s32[32]{0:T(128)}, u32[]{:S(2)}) copy-start(s32[32]{0:T(128)} %param.16) | copy-start | bytes 388
  7.2 245.9 %all-gather.3.cloned.1.call-start = ((), (), s32[]{:S(2)}) async-start(), calls=%async_computation.6 | async-start | bytes 8912896 | tf_op jit(solution)/shard_map/all_gather | solution.py:108
  10.3 408.4 %all-gather.5.cloned.1.call-start = ((), (), s32[]{:S(2)}) async-start(), calls=%async_computation.7 | async-start | bytes 8912896 | tf_op jit(solution)/shard_map/all_gather | solution.py:107
  61.8 59.6 %all-to-all-start.2 = ((bf16[32,32,256]{2,1,0:T(8,128)(2,1)}), bf16[32,32,256]{2,1,0:T(8,128)(2,1)S(1)}, u32[]{:S(2)}, u32[]{:S(2)}) async-start(bf16[32,32,256]{2,1,0:T(8,128)(2,1)} %bitcast.7), calls=%async_computation.2 | async-start | bytes 1048576 | tf_op jit(solution)/shard_map/all_to_all | solution.py:66
  121.4 70.4 %all-to-all-start.3 = ((bf16[32,8,1024]{2,1,0:T(8,128)(2,1)}), bf16[32,8,1024]{2,1,0:T(8,128)(2,1)S(1)}, u32[]{:S(2)}, u32[]{:S(2)}) async-start(bf16[32,8,1024]{2,1,0:T(8,128)(2,1)} %bitcast.8), calls=%async_computation.3 | async-start | bytes 1048576 | tf_op jit(solution)/shard_map/all_to_all | solution.py:67
  197.4 42.6 %all-to-all-start.4 = ((bf16[32,2,12288]{2,1,0:T(2,128)(2,1)}), bf16[32,2,12288]{2,1,0:T(2,128)(2,1)}, u32[]{:S(2)}, u32[]{:S(2)}) async-start(bf16[32,2,12288]{2,1,0:T(2,128)(2,1)} %reshape.318), calls=%async_computation.4 | async-start | bytes 3145728 | tf_op jit(solution)/shard_map/all_to_all | solution.py:14
  280.9 1.7 copy-start
  446.5 3.4 copy-start.2
  449.9 1.0 copy-start.1
  450.9 3.0 copy-start.12
  450.9 1.4 copy-start.8
  452.0 1.9 copy-start.14
  453.9 1.0 copy-start.3
  453.9 1.1 copy-start.5
  462.9 161.7 %all-to-all-start.5 = ((bf16[16,128,1024]{2,1,0:T(8,128)(2,1)}), bf16[16,128,1024]{2,1,0:T(8,128)(2,1)}, u32[]{:S(2)}, u32[]{:S(2)}) async-start(bf16[16,128,1024]{2,1,0:T(8,128)(2,1)} %copy.25), calls=%async_computation.5 | async-start | bytes 8388608 | tf_op jit(solution)/shard_map/all_to_all | solution.py:149
  467.9 3.1 copy-start.4
  471.0 1.8 copy-start.6
  472.9 1.8 copy-start.13
  472.9 1.9 copy-start.15
Sparse Core Ops, SparseCore 0:
  11.8 213.1 all-gather.2
  228.8 189.8 all-gather.4
where the time goes:
time: 646 us; the launch traced here: 637 us
  waiting for transfers between devices  360 us (56%)
  blocking collectives  104 us (16%)
  local copies, waits for them, and re-layouts  96.8 us (15%)
  starting transfers between devices  27 us (4%)
  matrix products  18.4 us (3%)
  between operations  15.3 us (2%)
  other arithmetic  14.8 us (2%)
    all_to_all x1, waiting for transfers between devices, on_device(): lax.all_to_all(slots, 'group', split_axis=0, concat_axis=0, tiled=True)  148 us
    all_gather x1, waiting for transfers between devices, on_device(): tok_piece = lax.all_gather(masked_tok, 'group', axis=0, tiled=True)  136 us
    gather x108, local copies, waits for them, and re-layouts  70 us
    all_to_all x1, waiting for transfers between devices, relocate(): lax.all_to_all(down_parts, 'node', split_axis=0, concat_axis=0, tiled=True)  54 us
    all_gather x1, blocking collectives, on_device(): lax.all_gather(router_gate.astype(jnp.bfloat16), 'group', axis=0, tiled=T...  53.6 us
    all_to_all x1, blocking collectives, sent_to_all(): return lax.all_to_all(copies, axis, split_axis=0, concat_axis=0, tiled=True)  27.9 us
    all_to_all x1, blocking collectives, relocate(): lax.all_to_all(gate_parts, 'node', split_axis=0, concat_axis=0, tiled=True)  22.8 us
    all_to_all x1, waiting for transfers between devices, side_by_side(): lax.all_to_all(both, axis, split_axis=split_dim, concat_axis=concat_dim,...  21.3 us
  transfers between devices with their start and end apart: 6, of which 4 were waited for; matrix products, arithmetic and copies ran while one was open for 12% of the time, Pallas kernels for 0%

commit v1 on v0

v1 whole, which is shorter than its diff:
```python
import functools

import jax
import jax.numpy as jnp
from jax import lax
from jax.experimental import pallas as pl
from jax.experimental.pallas import tpu as pltpu
from jax.sharding import PartitionSpec as P

BF = jnp.bfloat16
F32 = jnp.float32
MESH = pl.DeviceIdType.MESH
NODES = 32
GROUP = 16
RING = 8
BLK = 128
D = 1024
H = 256
HALF = D // 2
PART = 96


def slot(hops, way):
    if hops == 0:
        return 0
    return 7 if hops == RING // 2 else 2 * hops - 1 + way


def nt(left, right):
    return lax.dot_general(left, right, (((1,), (1,)), ((), ())), preferred_element_type=F32)


def tn(left, right):
    return lax.dot_general(left, right, (((0,), (0,)), ((), ())), preferred_element_type=F32)


def kernel(
    partner, meta_in, tok_in, gr_in, wg_in, wu_in, wd_in,
    dt_out, dg_out, du_out, dd_out,
    meta, tok, gr, xs, gs, gact, hact, cbuf, rbuf, sbuf, zsend, zrecv,
    pack, mixed, stage, wrec, dg_v, du_v, dd_v, dt_v,
    g_send, g_recv, m_send, m_recv, wa_send, wa_recv, wb_send, wb_recv,
    rs_send, rs_recv, z_send, z_recv, loc, out_sem,
):
    n = lax.axis_index("node")
    me = lax.axis_index("group")
    y = me // 2
    side = me % 2
    ring = (lax.rem(y + 1, RING) * 2 + side, lax.rem(y + RING - 1, RING) * 2 + side)
    mate = y * 2 + (1 - side)

    locals_ = [
        pltpu.make_async_copy(wg_in, pack.at[:, :, pl.ds(0, 32), :], loc.at[0]),
        pltpu.make_async_copy(wu_in, pack.at[:, :, pl.ds(32, 32), :], loc.at[1]),
    ]
    for cb in range(4):
        locals_.append(
            pltpu.make_async_copy(
                wd_in.at[:, :, pl.ds(256 * cb, 256)],
                pack.at[:, cb // 2, pl.ds(64 + 16 * (cb % 2), 16), :],
                loc.at[2 + cb],
            )
        )
    owns = [
        pltpu.make_async_copy(meta_in, meta.at[0], loc.at[6]),
        pltpu.make_async_copy(tok_in, tok.at[0], loc.at[7]),
        pltpu.make_async_copy(gr_in, gr.at[0], loc.at[8]),
    ]
    for c in locals_ + owns:
        c.start()

    barrier = pltpu.get_barrier_semaphore()

    def greet(k, carry):
        pl.semaphore_signal(
            barrier, inc=1, device_id=(lax.rem(n + k, NODES), me), device_id_type=MESH
        )
        return carry

    for g in (ring[0], ring[1], mate):
        pl.semaphore_signal(barrier, inc=1, device_id=(n, g), device_id_type=MESH)
    lax.fori_loop(1, NODES, greet, 0)
    pl.semaphore_wait(barrier, NODES - 1 + 3)

    bufs = (meta, tok, gr)
    ins = (meta_in, tok_in, gr_in)

    def gather(q, way, hops, c):
        src = ins[c] if q == 0 and hops == 1 else bufs[c].at[q * 8 + slot(hops - 1, way)]
        return pltpu.make_async_remote_copy(
            src_ref=src,
            dst_ref=bufs[c].at[q * 8 + slot(hops, way)],
            send_sem=g_send.at[q, way, hops - 1, c],
            recv_sem=g_recv.at[q, way, hops - 1, c],
            device_id=(n, ring[way]),
            device_id_type=MESH,
        )

    def has(way, hops, c):
        return hops < RING // 2 or (c == 2) == (way == 1)

    def to_mate(c):
        return pltpu.make_async_remote_copy(
            src_ref=ins[c],
            dst_ref=bufs[c].at[8],
            send_sem=m_send.at[c],
            recv_sem=m_recv.at[c],
            device_id=(n, mate),
            device_id_type=MESH,
        )

    def spread(k):
        to = lax.rem(n + k, NODES)
        return pltpu.make_async_remote_copy(
            src_ref=pack.at[to // 2, lax.rem(to, 2)],
            dst_ref=mixed.at[n],
            send_sem=wa_send.at[k],
            recv_sem=wa_recv.at[k],
            device_id=(to, me),
            device_id_type=MESH,
        )

    def collect(k):
        to = lax.rem(n + k, NODES)
        return pltpu.make_async_remote_copy(
            src_ref=stage.at[to],
            dst_ref=wrec.at[n],
            send_sem=wb_send.at[k],
            recv_sem=wb_recv.at[k],
            device_id=(to, me),
            device_id_type=MESH,
        )

    def each_peer(act):
        def body(k, carry):
            act(k)
            return carry

        lax.fori_loop(1, NODES, body, 0)

    def arrive(q, hops, c):
        for way in range(2):
            if has(way, hops, c):
                gather(q, way, hops, c).wait_recv()
                if hops < RING // 2 and has(way, hops + 1, c):
                    gather(q, way, hops + 1, c).start()

    def chosen_row(s):
        return meta[s, pl.ds(GROUP + me, 1), :]

    pick_me = (lax.broadcasted_iota(jnp.int32, (GROUP, 128), 0) == me).astype(F32)

    def compute(pair, carry):
        for j in range(2):
            s = 2 * pair + j
            second = chosen_row(s)
            first = 1.0 - second
            for cb in range(D // 128):
                cols = pl.ds(128 * cb, 128)
                for whole, sel in ((tok, xs), (gr, gs)):
                    a = whole[s, pl.ds(0, BLK), cols].astype(F32)
                    b = whole[s, pl.ds(BLK, BLK), cols].astype(F32)
                    sel[s, :, cols] = (a * first + b * second).astype(BF)
        two = pl.ds(2 * pair, 2)
        x = xs[two].reshape(2 * BLK, D)
        wg = wrec[:, pl.ds(0, 32), :].reshape(D, H)
        wu = wrec[:, pl.ds(32, 32), :].reshape(D, H)
        gate_pre = jnp.dot(x, wg, preferred_element_type=F32)
        up_pre = jnp.dot(x, wu, preferred_element_type=F32)
        grad_hidden = None
        for cb in range(4):
            g = gs[two, :, pl.ds(256 * cb, 256)].reshape(2 * BLK, 256)
            w = wd_block(cb)
            term = nt(g, w)
            grad_hidden = term if grad_hidden is None else grad_hidden + term
        weight = jnp.concatenate(
            [
                lax.dot_general(
                    meta[2 * pair + j, pl.ds(0, GROUP), :], pick_me, (((0,), (0,)), ((), ())),
                    preferred_element_type=F32, precision=lax.Precision.HIGHEST,
                )
                for j in range(2)
            ],
            axis=0,
        )
        weight = jnp.concatenate([weight, weight], axis=1)
        sig = 1.0 / (1.0 + jnp.exp(-gate_pre))
        swish = gate_pre * sig
        grad_hidden = grad_hidden * weight
        hact[two] = (swish * up_pre * weight).astype(BF).reshape(2, BLK, H)
        gu = (grad_hidden * swish).astype(BF)
        gg = (grad_hidden * up_pre * sig * (1.0 + gate_pre * (1.0 - sig))).astype(BF)
        gact[two, :, pl.ds(0, H)] = gg.reshape(2, BLK, H)
        gact[two, :, pl.ds(H, H)] = gu.reshape(2, BLK, H)
        back = nt(gg, wg) + nt(gu, wu)
        cbuf[two] = back.astype(BF).reshape(2, BLK, D)
        return carry

    def wd_block(cb):
        rows = pl.ds(64 + 16 * (cb % 2), 16)
        parts = [wrec[2 * i + cb // 2, rows, :] for i in range(16)]
        return jnp.concatenate(parts, axis=0)

    def run(first, last):
        lax.fori_loop(first, last, compute, 0)

    for c in range(3):
        for way in range(2):
            gather(0, way, 1, c).start()
    for c in locals_:
        c.wait()
    each_peer(lambda k: spread(k).start())
    for c in range(3):
        to_mate(c).start()
    mixed[n] = pack[n // 2, lax.rem(n, 2)]
    for c in range(3):
        arrive(0, 1, c)
    for c in range(3):
        arrive(0, 2, c)
    each_peer(lambda k: spread(k).wait_recv())

    def forward(k):
        to = lax.rem(n + k, NODES)
        stage[to] = mixed[partner[to]]
        collect(k).start()

    each_peer(forward)
    wrec[n] = mixed[partner[n]]
    for c in range(3):
        arrive(0, 3, c)
    for c in range(3):
        to_mate(c).wait_recv()
        for way in range(2):
            gather(1, way, 1, c).start()
    for c in range(3):
        arrive(0, 4, c)
    for c in owns:
        c.wait()
    for c in range(3):
        arrive(1, 1, c)
    each_peer(lambda k: collect(k).wait_recv())
    run(0, 1)
    for c in range(2):
        arrive(1, 2, c)
    run(1, 3)
    arrive(1, 2, 2)
    run(3, 6)
    for c in range(3):
        arrive(1, 3, c)
    run(6, 7)
    for c in range(3):
        arrive(1, 4, c)
    run(7, 8)

    outs = [
        pltpu.make_async_copy(dg_v, dg_out, out_sem.at[0]),
        pltpu.make_async_copy(du_v, du_out, out_sem.at[1]),
        pltpu.make_async_copy(dd_v, dd_out, out_sem.at[2]),
        pltpu.make_async_copy(dt_v, dt_out, out_sem.at[3]),
    ]

    def grad_piece(i):
        cols = pl.ds(256 * (i % 4), 256)
        if i < 4:
            x = xs[:, :, cols].reshape(GROUP * BLK, 256)
            both = tn(x, gact[...].reshape(GROUP * BLK, 2 * H))
            dg_v[cols, :] = both[:, :H].astype(BF)
            du_v[cols, :] = both[:, H:].astype(BF)
        else:
            g = gs[:, :, cols].reshape(GROUP * BLK, 256)
            dd_v[:, cols] = tn(hact[...].reshape(GROUP * BLK, H), g).astype(BF)
        if i == 3:
            outs[0].start()
            outs[1].start()
        if i == 7:
            outs[2].start()

    def term(s, c):
        row = chosen_row(s)
        second = jnp.concatenate([row] * (HALF // 128), axis=1)
        mine = cbuf[s, :, pl.ds(HALF * c, HALF)].astype(F32)
        return (mine * (1.0 - second), mine * second)

    def back_copy(q, way, hops, c):
        if hops == 4 or (hops == 3 and c != way):
            src = sbuf.at[q, way, 4 - hops]
        else:
            src = rbuf.at[q, way, hops, c]
        return pltpu.make_async_remote_copy(
            src_ref=src,
            dst_ref=rbuf.at[q, way, hops - 1, c],
            send_sem=rs_send.at[q, way, hops - 1, c],
            recv_sem=rs_recv.at[q, way, hops - 1, c],
            device_id=(n, ring[way]),
            device_id_type=MESH,
        )

    def back_send(q, way, hops, c):
        parts = term(q * 8 + slot(hops, 1 - way), c)
        if hops == 4 or (hops == 3 and c != way):
            for b in range(2):
                sbuf[q, way, 4 - hops, b] = parts[b].astype(BF)
        else:
            back_copy(q, way, hops + 1, c).wait_recv()
            for b in range(2):
                rbuf[q, way, hops, c, b] = (
                    rbuf[q, way, hops, c, b].astype(F32) + parts[b]
                ).astype(BF)
        back_copy(q, way, hops, c).start()

    steps = [
        (q, hops, turn)
        for q in (1, 0)
        for hops in (4, 3, 2, 1)
        for turn in range(2)
        if hops < 4 or turn == 0
    ]

    def z_copy(c):
        return pltpu.make_async_remote_copy(
            src_ref=zsend.at[c],
            dst_ref=zrecv.at[c],
            send_sem=z_send.at[c],
            recv_sem=z_recv.at[c],
            device_id=(n, mate),
            device_id_type=MESH,
        )

    def total(q, c):
        parts = term(q * 8, c)
        for way in range(2):
            back_copy(q, way, 1, c).wait_recv()
        return [
            parts[b] + rbuf[q, 0, 0, c, b].astype(F32) + rbuf[q, 1, 0, c, b].astype(F32)
            for b in range(2)
        ]

    for i, (q, hops, turn) in enumerate(steps):
        for way in range(2):
            back_send(q, way, hops, way ^ turn)
        if i < 8:
            grad_piece(i)
        if i == 7:
            for c in range(2):
                sums = total(1, c)
                for b in range(2):
                    zsend[c, b] = sums[b].astype(BF)
                z_copy(c).start()
    for c in range(2):
        sums = total(0, c)
        z_copy(c).wait_recv()
        for b in range(2):
            dt_v[pl.ds(BLK * b, BLK), pl.ds(HALF * c, HALF)] = (
                sums[b] + zrecv[c, b].astype(F32)
            ).astype(BF)
    outs[3].start()

    for q in range(2):
        for hops in range(1, 5):
            for c in range(3):
                for way in range(2):
                    if has(way, hops, c):
                        gather(q, way, hops, c).wait_send()
    for c in range(3):
        to_mate(c).wait_send()
    each_peer(lambda k: spread(k).wait_send())
    each_peer(lambda k: collect(k).wait_send())
    for q, hops, turn in steps:
        for way in range(2):
            back_copy(q, way, hops, way ^ turn).wait_send()
    for c in range(2):
        z_copy(c).wait_send()
    for c in outs:
        c.wait()


def on_device(tokens, grad_out, router_gate, counts, routes, partner, w_gate, w_up, w_down):
    groups = jnp.arange(GROUP, dtype=jnp.int32)
    live = jnp.arange(2, dtype=jnp.int32) < counts[0]
    gates = router_gate.T.reshape(4, 2, 1, BLK)
    hot = (routes[0].T[:, :, None] == groups) & live[None, :, None]
    weights = jnp.sum(jnp.where(hot[:, :, :, None], gates, 0.0), axis=(0, 1))
    second = jnp.any(routes[0, 1][:, None] == groups, axis=0).astype(F32)
    meta = jnp.concatenate([weights, jnp.broadcast_to(second[:, None], (GROUP, BLK))], axis=0)

    any_ = pl.BlockSpec(memory_space=pl.ANY)
    dma = pltpu.SemaphoreType.DMA
    shape = jax.ShapeDtypeStruct
    outs = pl.pallas_call(
        kernel,
        out_shape=(
            shape((2 * BLK, D), BF), shape((D, H), BF), shape((D, H), BF), shape((H, D), BF),
        ),
        in_specs=[pl.BlockSpec(memory_space=pltpu.SMEM)] + [any_] * 6,
        out_specs=[any_] * 4,
        scratch_shapes=[
            pltpu.VMEM((16, 32, 128), F32),
            pltpu.VMEM((16, 2 * BLK, D), BF),
            pltpu.VMEM((16, 2 * BLK, D), BF),
            pltpu.VMEM((16, BLK, D), BF),
            pltpu.VMEM((16, BLK, D), BF),
            pltpu.VMEM((16, BLK, 2 * H), BF),
            pltpu.VMEM((16, BLK, H), BF),
            pltpu.VMEM((16, BLK, D), BF),
            pltpu.VMEM((2, 2, 4, 2, 2, BLK, HALF), BF),
            pltpu.VMEM((2, 2, 2, 2, BLK, HALF), BF),
            pltpu.VMEM((2, 2, BLK, HALF), BF),
            pltpu.VMEM((2, 2, BLK, HALF), BF),
            pltpu.VMEM((16, 2, PART, H), BF),
            pltpu.VMEM((NODES, PART, H), BF),
            pltpu.VMEM((NODES, PART, H), BF),
            pltpu.VMEM((NODES, PART, H), BF),
            pltpu.VMEM((D, H), BF),
            pltpu.VMEM((D, H), BF),
            pltpu.VMEM((H, D), BF),
            pltpu.VMEM((2 * BLK, D), BF),
            dma((2, 2, 4, 3)), dma((2, 2, 4, 3)), dma((3,)), dma((3,)),
            dma((NODES,)), dma((NODES,)), dma((NODES,)), dma((NODES,)),
            dma((2, 2, 4, 2)), dma((2, 2, 4, 2)), dma((2,)), dma((2,)), dma((9,)), dma((4,)),
        ],
        compiler_params=pltpu.CompilerParams(
            collective_id=0, has_side_effects=True, vmem_limit_bytes=67043328
        ),
        name="moe_step",
    )(
        partner, meta, tokens, grad_out,
        w_gate.reshape(16, 2, 32, H), w_up.reshape(16, 2, 32, H), w_down.reshape(16, 16, D),
    )
    dt, dg, du, dd = outs
    return dt, dg.reshape(1, D, H), du.reshape(1, D, H), dd.reshape(1, H, D)


def solution(mesh):
    rows = P(("node", "group"), None)
    cube = P(("node", "group"), None, None)
    return jax.shard_map(
        on_device,
        mesh=mesh,
        in_specs=(rows, rows, rows, P(("node", "group")), cube, P(), cube, cube, cube),
        out_specs=(rows, cube, cube, cube),
        check_vma=False,
    )
```

time: 646 us -> 302 us (0.47)
  the two profiles are of different devices: /device:TPU:6 before, /device:TPU:350 now
where the time goes in v1:
time: 302 us
  Pallas kernels  293 us (97%)
  local copies, waits for them, and re-layouts  6.56 us (2%)
    pallas_call x1, Pallas kernels, on_device(): pl.pallas_call(kernel, out_shape=(shape((2 * BLK, D), BF), shape((D, H),...  293 us
    unnamed x14, local copies, waits for them, and re-layouts  6.37 us

profile of v1, /device:TPU:350, one launch (start us, length us, event | category | flops | bytes accessed | tf_op | source)
XLA Modules:
  0.0 301.9 jit_solution(7191689167670953999)
XLA Ops:
  1.3 0.0 copy-start.4
  1.3 0.7 copy-done.4
  2.0 0.1 fusion
  2.1 0.1 pad.1.clone
  2.2 0.0 copy-start.3
  2.2 0.1 copy.14
  2.2 0.1 compare_and_fusion
  2.3 0.5 copy-done.3
  2.9 0.1 select_reduce_fusion
  2.9 0.7 pad_maximum_fusion.meta_in
  3.6 293.0 %moe_step.1 = (bf16[256,1024]{1,0:T(8,128)(2,1)}, bf16[1024,256]{1,0:T(8,128)(2,1)}, bf16[1024,256]{1,0:T(8,128)(2,1)}, bf16[256,1024]{1,0:T(8,128)(2,1)}) custom-call(s32[32]{0:T(128)} %partner.1, f32[32,128]{1,0:T(8,128)} %pad_maximum_fusion.meta_in, bf16[256,1024]{1,0:T(8,128)(2,1)} %tok_in.1, bf16[256,1024]{1,0:T(8,128)(2,1)} %gr_in.1, ...), custom_call_target="tpu_custom_call" | custom-call | tf_op jit(solution)/shard_map/moe_step/pallas_call | solution.py:389
  296.7 0.0 copy-start.2
  296.7 1.9 copy.20
  298.6 0.0 copy-done.2
  298.6 0.0 copy-start.1
  298.6 0.8 copy.21
  299.4 0.4 copy-done.1
  299.8 0.0 copy-start
  299.9 0.8 copy.22
  300.6 0.4 copy-done
  301.1 0.8 copy.23
  (4 shorter events, 0.0 us)
Async XLA Ops:
  1.3 0.7 copy-start.4
  2.2 0.7 copy-start.3
  296.7 1.9 copy-start.2
  298.6 1.2 copy-start.1
  299.8 1.2 copy-start

commit v2 on v1

--- a/solution.py
+++ b/solution.py
@@ -37,10 +37,10 @@
 def kernel(
     partner, meta_in, tok_in, gr_in, wg_in, wu_in, wd_in,
     dt_out, dg_out, du_out, dd_out,
-    meta, tok, gr, xs, gs, gact, hact, cbuf, rbuf, sbuf, zsend, zrecv,
+    meta, tok, gr, xs, gs, gact, hact, cbuf, cut, relay, zrel, raw, near, far, sbuf, rbuf, zsend, zrecv, zmeta,
     pack, mixed, stage, wrec, dg_v, du_v, dd_v, dt_v,
-    g_send, g_recv, m_send, m_recv, wa_send, wa_recv, wb_send, wb_recv,
-    rs_send, rs_recv, z_send, z_recv, loc, out_sem,
+    g_send, g_recv, s_send, s_recv, m_send, m_recv, wa_send, wa_recv, wb_send, wb_recv,
+    r_send, r_recv, rs_send, rs_recv, z_send, z_recv, loc, out_sem,
 ):
     n = lax.axis_index("node")
     me = lax.axis_index("group")
@@ -48,6 +48,9 @@
     side = me % 2
     ring = (lax.rem(y + 1, RING) * 2 + side, lax.rem(y + RING - 1, RING) * 2 + side)
     mate = y * 2 + (1 - side)
+    turned = (n >= NODES // 2).astype(jnp.int32)
+    zside = (y * 2 + lax.rem(side + turned, 2), y * 2 + lax.rem(side + 1 - turned, 2))
+    beyond = (lax.rem(y + 2, RING) * 2 + side, lax.rem(y + RING - 2, RING) * 2 + side)
 
     locals_ = [
         pltpu.make_async_copy(wg_in, pack.at[:, :, pl.ds(0, 32), :], loc.at[0]),
@@ -62,9 +65,9 @@
             )
         )
     owns = [
-        pltpu.make_async_copy(meta_in, meta.at[0], loc.at[6]),
-        pltpu.make_async_copy(tok_in, tok.at[0], loc.at[7]),
-        pltpu.make_async_copy(gr_in, gr.at[0], loc.at[8]),
+        pltpu.make_async_copy(meta_in, meta.at[0, 0], loc.at[6]),
+        pltpu.make_async_copy(tok_in, tok.at[0, 0], loc.at[7]),
+        pltpu.make_async_copy(gr_in, gr.at[0, 0], loc.at[8]),
     ]
     for c in locals_ + owns:
         c.start()
@@ -80,32 +83,57 @@
     for g in (ring[0], ring[1], mate):
         pl.semaphore_signal(barrier, inc=1, device_id=(n, g), device_id_type=MESH)
     lax.fori_loop(1, NODES, greet, 0)
-    pl.semaphore_wait(barrier, NODES - 1 + 3)
+    pl.semaphore_signal(
+        barrier, inc=1, device_id=(lax.rem(n + NODES // 2, NODES), mate), device_id_type=MESH
+    )
+    pl.semaphore_wait(barrier, NODES - 1 + 4)
 
     bufs = (meta, tok, gr)
     ins = (meta_in, tok_in, gr_in)
 
     def gather(q, way, hops, c):
-        src = ins[c] if q == 0 and hops == 1 else bufs[c].at[q * 8 + slot(hops - 1, way)]
+        src = ins[c] if q == 0 and hops == 1 else bufs[c].at[q, slot(hops - 1, way)]
         return pltpu.make_async_remote_copy(
             src_ref=src,
-            dst_ref=bufs[c].at[q * 8 + slot(hops, way)],
+            dst_ref=bufs[c].at[q, slot(hops, way)],
             send_sem=g_send.at[q, way, hops - 1, c],
             recv_sem=g_recv.at[q, way, hops - 1, c],
             device_id=(n, ring[way]),
             device_id_type=MESH,
         )
 
-    def has(way, hops, c):
-        return hops < RING // 2 or (c == 2) == (way == 1)
-
-    def to_mate(c):
-        return pltpu.make_async_remote_copy(
-            src_ref=ins[c],
-            dst_ref=bufs[c].at[8],
-            send_sem=m_send.at[c],
-            recv_sem=m_recv.at[c],
-            device_id=(n, mate),
+    def cut_copy(q, way, k):
+        if k < 2:
+            dst = (xs, gs)[k].at[q * 8 + slot(3, way)]
+        else:
+            dst = relay.at[q, way]
+        return pltpu.make_async_remote_copy(
+            src_ref=cut.at[q, way, k],
+            dst_ref=dst,
+            send_sem=s_send.at[q, way, k],
+            recv_sem=s_recv.at[q, way, k],
+            device_id=(n, ring[way]),
+            device_id_type=MESH,
+        )
+
+    def last_copy(q, way):
+        return pltpu.make_async_remote_copy(
+            src_ref=relay.at[q, way],
+            dst_ref=(xs, gs)[way].at[q * 8 + 7],
+            send_sem=s_send.at[q, way, 3],
+            recv_sem=s_recv.at[q, way, 3],
+            device_id=(n, ring[way]),
+            device_id_type=MESH,
+        )
+
+    def to_mate(c, leg):
+        stop = zrel.at[c - 1] if c else zmeta
+        return pltpu.make_async_remote_copy(
+            src_ref=ins[c] if leg == 0 else stop,
+            dst_ref=stop if leg == 0 else bufs[c].at[1, 0],
+            send_sem=m_send.at[c, leg],
+            recv_sem=m_recv.at[c, leg],
+            device_id=(lax.rem(n + NODES // 2, NODES), zside[1 if c == 2 else 0]),
             device_id_type=MESH,
         )
 
@@ -138,29 +166,53 @@
 
         lax.fori_loop(1, NODES, body, 0)
 
+    def row_of(q, r, who):
+        return meta[q, r, pl.ds(GROUP + who, 1), :]
+
+    def choose(q, r, c, who, dst):
+        second = row_of(q, r, who)
+        first = 1.0 - second
+        for cb in range(D // 128):
+            cols = pl.ds(128 * cb, 128)
+            a = bufs[c][q, r, pl.ds(0, BLK), cols].astype(F32)
+            b = bufs[c][q, r, pl.ds(BLK, BLK), cols].astype(F32)
+            dst[:, cols] = (a * first + b * second).astype(BF)
+
     def arrive(q, hops, c):
-        for way in range(2):
-            if has(way, hops, c):
-                gather(q, way, hops, c).wait_recv()
-                if hops < RING // 2 and has(way, hops + 1, c):
-                    gather(q, way, hops + 1, c).start()
-
-    def chosen_row(s):
-        return meta[s, pl.ds(GROUP + me, 1), :]
+        if hops == 1:
+            for way in range(2):
+                gather(q, way, 1, c).wait_recv()
+                gather(q, way, 2, c).start()
+        elif hops == 2:
+            for way in range(2):
+                gather(q, way, 2, c).wait_recv()
+                if c == 0:
+                    gather(q, way, 3, 0).start()
+                    continue
+                if c == 1 + way:
+                    choose(q, slot(2, way), c, beyond[way], cut.at[q, way, 2])
+                    cut_copy(q, way, 2).start()
+                choose(q, slot(2, way), c, ring[way], cut.at[q, way, c - 1])
+                cut_copy(q, way, c - 1).start()
+        elif hops == 3:
+            for way in range(2):
+                if c == 0:
+                    gather(q, way, 3, 0).wait_recv()
+                    if way == 0:
+                        gather(q, way, 4, 0).start()
+                    continue
+                if c == 1 + way:
+                    cut_copy(q, way, 2).wait_recv()
+                    last_copy(q, way).start()
+                cut_copy(q, way, c - 1).wait_recv()
+        elif c == 0:
+            gather(q, 0, 4, 0).wait_recv()
+        else:
+            last_copy(q, c - 1).wait_recv()
 
     pick_me = (lax.broadcasted_iota(jnp.int32, (GROUP, 128), 0) == me).astype(F32)
 
     def compute(pair, carry):
-        for j in range(2):
-            s = 2 * pair + j
-            second = chosen_row(s)
-            first = 1.0 - second
-            for cb in range(D // 128):
-                cols = pl.ds(128 * cb, 128)
-                for whole, sel in ((tok, xs), (gr, gs)):
-                    a = whole[s, pl.ds(0, BLK), cols].astype(F32)
-                    b = whole[s, pl.ds(BLK, BLK), cols].astype(F32)
-                    sel[s, :, cols] = (a * first + b * second).astype(BF)
         two = pl.ds(2 * pair, 2)
         x = xs[two].reshape(2 * BLK, D)
         wg = wrec[:, pl.ds(0, 32), :].reshape(D, H)
@@ -176,7 +228,7 @@
         weight = jnp.concatenate(
             [
                 lax.dot_general(
-                    meta[2 * pair + j, pl.ds(0, GROUP), :], pick_me, (((0,), (0,)), ((), ())),
+                    meta[pair // 4, 2 * lax.rem(pair, 4) + j, pl.ds(0, GROUP), :], pick_me, (((0,), (0,)), ((), ())),
                     preferred_element_type=F32, precision=lax.Precision.HIGHEST,
                 )
                 for j in range(2)
@@ -204,19 +256,68 @@
     def run(first, last):
         lax.fori_loop(first, last, compute, 0)
 
+    def pick(q, first, last):
+        def body(r, carry):
+            for c, sel in ((1, xs), (2, gs)):
+                choose(q, r, c, me, sel.at[q * 8 + r])
+            return carry
+
+        lax.fori_loop(first, last, body, 0)
+
+    def raw_copy(q, way, k):
+        if k == 2:
+            src, dst = cbuf.at[q * 8 + 7, :, pl.ds(HALF * way, HALF)], near.at[q, way]
+        elif k == 3:
+            src, dst = near.at[q, way], far.at[q, way]
+        else:
+            src = cbuf.at[q * 8 + slot(3, 1 - way), :, pl.ds(HALF * k, HALF)]
+            dst = raw.at[q, way, k]
+        return pltpu.make_async_remote_copy(
+            src_ref=src,
+            dst_ref=dst,
+            send_sem=r_send.at[q, way, k],
+            recv_sem=r_recv.at[q, way, k],
+            device_id=(n, ring[way]),
+            device_id_type=MESH,
+        )
+
     for c in range(3):
         for way in range(2):
             gather(0, way, 1, c).start()
+    for c in range(3):
+        to_mate(c, 0).start()
     for c in locals_:
         c.wait()
+    mixed[n] = pack[n // 2, lax.rem(n, 2)]
+    for c in owns:
+        c.wait()
+    pick(0, 0, 1)
+    for c in range(2):
+        arrive(0, 1, c)
+    for c in range(2):
+        to_mate(c, 0).wait_recv()
+        to_mate(c, 1).start()
+    arrive(0, 1, 2)
+    to_mate(2, 0).wait_recv()
+    to_mate(2, 1).start()
     each_peer(lambda k: spread(k).start())
-    for c in range(3):
-        to_mate(c).start()
-    mixed[n] = pack[n // 2, lax.rem(n, 2)]
-    for c in range(3):
-        arrive(0, 1, c)
+    pick(0, 1, 3)
     for c in range(3):
         arrive(0, 2, c)
+    pick(0, 3, 5)
+    for c in range(2):
+        arrive(0, 3, c)
+    for c in range(2):
+        to_mate(c, 1).wait_recv()
+        for way in range(2):
+            gather(1, way, 1, c).start()
+    arrive(0, 3, 2)
+    to_mate(2, 1).wait_recv()
+    for way in range(2):
+        gather(1, way, 1, 2).start()
+    pick(1, 0, 1)
+    for c in range(3):
+        arrive(0, 4, c)
     each_peer(lambda k: spread(k).wait_recv())
 
     def forward(k):
@@ -227,27 +328,21 @@
     each_peer(forward)
     wrec[n] = mixed[partner[n]]
     for c in range(3):
-        arrive(0, 3, c)
-    for c in range(3):
-        to_mate(c).wait_recv()
-        for way in range(2):
-            gather(1, way, 1, c).start()
-    for c in range(3):
-        arrive(0, 4, c)
-    for c in owns:
-        c.wait()
-    for c in range(3):
         arrive(1, 1, c)
+    pick(1, 1, 3)
+    for c in range(3):
+        arrive(1, 2, c)
+    pick(1, 3, 5)
     each_peer(lambda k: collect(k).wait_recv())
-    run(0, 1)
-    for c in range(2):
-        arrive(1, 2, c)
-    run(1, 3)
-    arrive(1, 2, 2)
-    run(3, 6)
-    for c in range(3):
+    run(0, 2)
+    for c in range(2):
         arrive(1, 3, c)
-    run(6, 7)
+    run(2, 4)
+    arrive(1, 3, 2)
+    for way in range(2):
+        for k in (2, 0, 1):
+            raw_copy(0, way, k).start()
+    run(4, 7)
     for c in range(3):
         arrive(1, 4, c)
     run(7, 8)
@@ -275,19 +370,20 @@
         if i == 7:
             outs[2].start()
 
-    def term(s, c):
-        row = chosen_row(s)
-        second = jnp.concatenate([row] * (HALF // 128), axis=1)
-        mine = cbuf[s, :, pl.ds(HALF * c, HALF)].astype(F32)
-        return (mine * (1.0 - second), mine * second)
+    def wide(row):
+        return jnp.concatenate([row] * (HALF // 128), axis=1)
+
+    def placed(block, row):
+        second = wide(row)
+        block = block.astype(F32)
+        return (block * (1.0 - second), block * second)
+
+    def term(q, r, c):
+        return placed(cbuf[q * 8 + r, :, pl.ds(HALF * c, HALF)], row_of(q, r, me))
 
     def back_copy(q, way, hops, c):
-        if hops == 4 or (hops == 3 and c != way):
-            src = sbuf.at[q, way, 4 - hops]
-        else:
-            src = rbuf.at[q, way, hops, c]
-        return pltpu.make_async_remote_copy(
-            src_ref=src,
+        return pltpu.make_async_remote_copy(
+            src_ref=sbuf.at[q, way, c] if hops == 2 else rbuf.at[q, way, 1, c],
             dst_ref=rbuf.at[q, way, hops - 1, c],
             send_sem=rs_send.at[q, way, hops - 1, c],
             recv_sem=rs_recv.at[q, way, hops - 1, c],
@@ -296,16 +392,33 @@
         )
 
     def back_send(q, way, hops, c):
-        parts = term(q * 8 + slot(hops, 1 - way), c)
-        if hops == 4 or (hops == 3 and c != way):
+        r = slot(hops, 1 - way)
+        if hops == 4:
+            if q == 1:
+                raw_copy(q, way, 2).start()
+            return
+        if hops == 3:
+            if c == way:
+                raw_copy(q, way, 2).wait_recv()
+                raw_copy(q, way, 3).start()
+            if q == 1:
+                raw_copy(q, way, c).start()
+            return
+        sums = term(q, r, c)
+        if hops == 2:
+            raw_copy(q, way, c).wait_recv()
+            more = placed(raw[q, way, c], row_of(q, r, ring[1 - way]))
+            sums = [u + v for u, v in zip(sums, more)]
+            if c == way:
+                raw_copy(q, way, 3).wait_recv()
+                more = placed(far[q, way], row_of(q, r, beyond[1 - way]))
+                sums = [u + v for u, v in zip(sums, more)]
             for b in range(2):
-                sbuf[q, way, 4 - hops, b] = parts[b].astype(BF)
+                sbuf[q, way, c, b] = sums[b].astype(BF)
         else:
-            back_copy(q, way, hops + 1, c).wait_recv()
+            back_copy(q, way, 2, c).wait_recv()
             for b in range(2):
-                rbuf[q, way, hops, c, b] = (
-                    rbuf[q, way, hops, c, b].astype(F32) + parts[b]
-                ).astype(BF)
+                rbuf[q, way, 1, c, b] = (rbuf[q, way, 1, c, b].astype(F32) + sums[b]).astype(BF)
         back_copy(q, way, hops, c).start()
 
     steps = [
@@ -327,7 +440,7 @@
         )
 
     def total(q, c):
-        parts = term(q * 8, c)
+        parts = term(q, 0, c)
         for way in range(2):
             back_copy(q, way, 1, c).wait_recv()
         return [
@@ -356,18 +469,25 @@
     outs[3].start()
 
     for q in range(2):
-        for hops in range(1, 5):
+        for way in range(2):
             for c in range(3):
-                for way in range(2):
-                    if has(way, hops, c):
-                        gather(q, way, hops, c).wait_send()
-    for c in range(3):
-        to_mate(c).wait_send()
+                gather(q, way, 1, c).wait_send()
+                gather(q, way, 2, c).wait_send()
+                cut_copy(q, way, c).wait_send()
+            gather(q, way, 3, 0).wait_send()
+            if way == 0:
+                gather(q, way, 4, 0).wait_send()
+            last_copy(q, way).wait_send()
+            for k in range(4):
+                raw_copy(q, way, k).wait_send()
+            for hops in (2, 1):
+                for c in range(2):
+                    back_copy(q, way, hops, c).wait_send()
+    for c in range(3):
+        for leg in range(2):
+            to_mate(c, leg).wait_send()
     each_peer(lambda k: spread(k).wait_send())
     each_peer(lambda k: collect(k).wait_send())
-    for q, hops, turn in steps:
-        for way in range(2):
-            back_copy(q, way, hops, way ^ turn).wait_send()
     for c in range(2):
         z_copy(c).wait_send()
     for c in outs:
@@ -394,18 +514,25 @@
         in_specs=[pl.BlockSpec(memory_space=pltpu.SMEM)] + [any_] * 6,
         out_specs=[any_] * 4,
         scratch_shapes=[
-            pltpu.VMEM((16, 32, 128), F32),
-            pltpu.VMEM((16, 2 * BLK, D), BF),
-            pltpu.VMEM((16, 2 * BLK, D), BF),
+            pltpu.VMEM((2, 8, 32, 128), F32),
+            pltpu.VMEM((2, 5, 2 * BLK, D), BF),
+            pltpu.VMEM((2, 5, 2 * BLK, D), BF),
             pltpu.VMEM((16, BLK, D), BF),
             pltpu.VMEM((16, BLK, D), BF),
             pltpu.VMEM((16, BLK, 2 * H), BF),
             pltpu.VMEM((16, BLK, H), BF),
             pltpu.VMEM((16, BLK, D), BF),
-            pltpu.VMEM((2, 2, 4, 2, 2, BLK, HALF), BF),
-            pltpu.VMEM((2, 2, 2, 2, BLK, HALF), BF),
+            pltpu.VMEM((2, 2, 3, BLK, D), BF),
+            pltpu.VMEM((2, 2, BLK, D), BF),
+            pltpu.VMEM((2, 2 * BLK, D), BF),
+            pltpu.VMEM((2, 2, 2, BLK, HALF), BF),
             pltpu.VMEM((2, 2, BLK, HALF), BF),
             pltpu.VMEM((2, 2, BLK, HALF), BF),
+            pltpu.VMEM((2, 2, 2, 2, BLK, HALF), BF),
+            pltpu.VMEM((2, 2, 2, 2, 2, BLK, HALF), BF),
+            pltpu.VMEM((2, 2, BLK, HALF), BF),
+            pltpu.VMEM((2, 2, BLK, HALF), BF),
+            pltpu.VMEM((32, 128), F32),
             pltpu.VMEM((16, 2, PART, H), BF),
             pltpu.VMEM((NODES, PART, H), BF),
             pltpu.VMEM((NODES, PART, H), BF),
@@ -414,9 +541,9 @@
             pltpu.VMEM((D, H), BF),
             pltpu.VMEM((H, D), BF),
             pltpu.VMEM((2 * BLK, D), BF),
-            dma((2, 2, 4, 3)), dma((2, 2, 4, 3)), dma((3,)), dma((3,)),
+            dma((2, 2, 4, 3)), dma((2, 2, 4, 3)), dma((2, 2, 4)), dma((2, 2, 4)), dma((3, 2)), dma((3, 2)),
             dma((NODES,)), dma((NODES,)), dma((NODES,)), dma((NODES,)),
-            dma((2, 2, 4, 2)), dma((2, 2, 4, 2)), dma((2,)), dma((2,)), dma((9,)), dma((4,)),
+            dma((2, 2, 4)), dma((2, 2, 4)), dma((2, 2, 2, 2)), dma((2, 2, 2, 2)), dma((2,)), dma((2,)), dma((9,)), dma((4,)),
         ],
         compiler_params=pltpu.CompilerParams(
             collective_id=0, has_side_effects=True, vmem_limit_bytes=67043328

time: 302 us -> 253 us (0.84)
  the two profiles are of different devices: /device:TPU:350 before, /device:TPU:70 now
where the time goes in v2:
time: 253 us; the launch traced here: 252 us
  Pallas kernels  243 us (96%)
  local copies, waits for them, and re-layouts  6.56 us (3%)
    pallas_call x1, Pallas kernels, on_device(): pl.pallas_call(kernel, out_shape=(shape((2 * BLK, D), BF), shape((D, H),...  243 us
    unnamed x14, local copies, waits for them, and re-layouts  6.37 us

profile of v2, /device:TPU:70, one launch (start us, length us, event | category | flops | bytes accessed | tf_op | source)
XLA Modules:
  0.0 252.3 jit_solution(9012961363067814093)
XLA Ops:
  1.3 0.0 copy-start.4
  1.3 0.7 copy-done.4
  2.0 0.1 fusion
  2.1 0.1 pad.1.clone
  2.2 0.0 copy-start.3
  2.2 0.1 copy.14
  2.2 0.1 compare_and_fusion
  2.3 0.5 copy-done.3
  2.9 0.1 select_reduce_fusion
  2.9 0.7 pad_maximum_fusion.meta_in
  3.6 243.4 %moe_step.1 = (bf16[256,1024]{1,0:T(8,128)(2,1)}, bf16[1024,256]{1,0:T(8,128)(2,1)}, bf16[1024,256]{1,0:T(8,128)(2,1)}, bf16[256,1024]{1,0:T(8,128)(2,1)}) custom-call(s32[32]{0:T(128)} %partner.1, f32[32,128]{1,0:T(8,128)} %pad_maximum_fusion.meta_in, bf16[256,1024]{1,0:T(8,128)(2,1)} %tok_in.1, bf16[256,1024]{1,0:T(8,128)(2,1)} %gr_in.1, ...), custom_call_target="tpu_custom_call" | custom-call | tf_op jit(solution)/shard_map/moe_step/pallas_call | solution.py:509
  247.1 0.0 copy-start.2
  247.1 1.9 copy.20
  249.0 0.0 copy-done.2
  249.0 0.0 copy-start.1
  249.0 0.8 copy.21
  249.8 0.4 copy-done.1
  250.2 0.0 copy-start
  250.2 0.8 copy.22
  251.0 0.4 copy-done
  251.5 0.8 copy.23
  (4 shorter events, 0.0 us)
Async XLA Ops:
  1.3 0.7 copy-start.4
  2.2 0.7 copy-start.3
  247.1 1.9 copy-start.2
  249.0 1.2 copy-start.1
  250.2 1.2 copy-start

commit v3 on v2

--- a/solution.py
+++ b/solution.py
@@ -16,7 +16,9 @@
 BLK = 128
 D = 1024
 H = 256
-HALF = D // 2
+XW = 640
+XC = ((0, 384), (384, 256))
+ZC = ((640, 256), (896, 128))
 PART = 96
 
 
@@ -37,10 +39,11 @@
 def kernel(
     partner, meta_in, tok_in, gr_in, wg_in, wu_in, wd_in,
     dt_out, dg_out, du_out, dd_out,
-    meta, tok, gr, xs, gs, gact, hact, cbuf, cut, relay, zrel, raw, near, far, sbuf, rbuf, zsend, zrecv, zmeta,
+    meta, tok, gr, xs, gs, gact, hact, cbuf, cut, relay, zrel, zmeta,
+    raw, near, far, sbuf, rbuf, zst, zr, zf, cm, zsend, zl, zrecv,
     pack, mixed, stage, wrec, dg_v, du_v, dd_v, dt_v,
     g_send, g_recv, s_send, s_recv, m_send, m_recv, wa_send, wa_recv, wb_send, wb_recv,
-    r_send, r_recv, rs_send, rs_recv, z_send, z_recv, loc, out_sem,
+    r_send, r_recv, rs_send, rs_recv, t_send, t_recv, f_send, f_recv, z_send, z_recv, loc, out_sem,
 ):
     n = lax.axis_index("node")
     me = lax.axis_index("group")
@@ -80,13 +83,13 @@
         )
         return carry
 
-    for g in (ring[0], ring[1], mate):
+    for g in ring:
         pl.semaphore_signal(barrier, inc=1, device_id=(n, g), device_id_type=MESH)
     lax.fori_loop(1, NODES, greet, 0)
     pl.semaphore_signal(
         barrier, inc=1, device_id=(lax.rem(n + NODES // 2, NODES), mate), device_id_type=MESH
     )
-    pl.semaphore_wait(barrier, NODES - 1 + 4)
+    pl.semaphore_wait(barrier, NODES - 1 + 3)
 
     bufs = (meta, tok, gr)
     ins = (meta_in, tok_in, gr_in)
@@ -137,8 +140,11 @@
             device_id_type=MESH,
         )
 
+    def flip(k):
+        return sum(lax.rem(n // (1 << i) + k // (1 << i), 2) * (1 << i) for i in range(5))
+
     def spread(k):
-        to = lax.rem(n + k, NODES)
+        to = flip(k)
         return pltpu.make_async_remote_copy(
             src_ref=pack.at[to // 2, lax.rem(to, 2)],
             dst_ref=mixed.at[n],
@@ -149,7 +155,7 @@
         )
 
     def collect(k):
-        to = lax.rem(n + k, NODES)
+        to = flip(k)
         return pltpu.make_async_remote_copy(
             src_ref=stage.at[to],
             dst_ref=wrec.at[n],
@@ -167,7 +173,7 @@
         lax.fori_loop(1, NODES, body, 0)
 
     def row_of(q, r, who):
-        return meta[q, r, pl.ds(GROUP + who, 1), :]
+        return (meta[q, r, pl.ds(who, 1), :] < 0.0).astype(F32)
 
     def choose(q, r, c, who, dst):
         second = row_of(q, r, who)
@@ -228,14 +234,14 @@
         weight = jnp.concatenate(
             [
                 lax.dot_general(
-                    meta[pair // 4, 2 * lax.rem(pair, 4) + j, pl.ds(0, GROUP), :], pick_me, (((0,), (0,)), ((), ())),
+                    meta[pair // 4, 2 * lax.rem(pair, 4) + j], pick_me, (((0,), (0,)), ((), ())),
                     preferred_element_type=F32, precision=lax.Precision.HIGHEST,
                 )
                 for j in range(2)
             ],
             axis=0,
         )
-        weight = jnp.concatenate([weight, weight], axis=1)
+        weight = jnp.abs(jnp.concatenate([weight, weight], axis=1))
         sig = 1.0 / (1.0 + jnp.exp(-gate_pre))
         swish = gate_pre * sig
         grad_hidden = grad_hidden * weight
@@ -265,13 +271,13 @@
         lax.fori_loop(first, last, body, 0)
 
     def raw_copy(q, way, k):
+        cols = pl.ds(*XC[k if k < 2 else way])
         if k == 2:
-            src, dst = cbuf.at[q * 8 + 7, :, pl.ds(HALF * way, HALF)], near.at[q, way]
+            src, dst = cbuf.at[q * 8 + 7, :, cols], near.at[q, way, :, cols]
         elif k == 3:
-            src, dst = near.at[q, way], far.at[q, way]
+            src, dst = near.at[q, way, :, cols], far.at[q, way, :, cols]
         else:
-            src = cbuf.at[q * 8 + slot(3, 1 - way), :, pl.ds(HALF * k, HALF)]
-            dst = raw.at[q, way, k]
+            src, dst = cbuf.at[q * 8 + slot(3, 1 - way), :, cols], raw.at[q, way, :, cols]
         return pltpu.make_async_remote_copy(
             src_ref=src,
             dst_ref=dst,
@@ -280,6 +286,21 @@
             device_id=(n, ring[way]),
             device_id_type=MESH,
         )
+
+    def across(r, leg):
+        return pltpu.make_async_remote_copy(
+            src_ref=zf.at[r] if leg else cbuf.at[8 + r, :, pl.ds(XW, D - XW)],
+            dst_ref=cm.at[r] if leg else zf.at[r],
+            send_sem=f_send.at[r, leg],
+            recv_sem=f_recv.at[r, leg],
+            device_id=(lax.rem(n + NODES // 2, NODES), zside[r % 2]),
+            device_id_type=MESH,
+        )
+
+    def hand_across(first, last):
+        for r in range(first, last):
+            across(r, 0).wait_recv()
+            across(r, 1).start()
 
     for c in range(3):
         for way in range(2):
@@ -321,7 +342,7 @@
     each_peer(lambda k: spread(k).wait_recv())
 
     def forward(k):
-        to = lax.rem(n + k, NODES)
+        to = flip(k)
         stage[to] = mixed[partner[to]]
         collect(k).start()
 
@@ -342,7 +363,12 @@
     for way in range(2):
         for k in (2, 0, 1):
             raw_copy(0, way, k).start()
-    run(4, 7)
+    run(4, 6)
+    for r in range(4):
+        across(r, 0).start()
+    run(6, 7)
+    for r in range(4, 6):
+        across(r, 0).start()
     for c in range(3):
         arrive(1, 4, c)
     run(7, 8)
@@ -370,21 +396,26 @@
         if i == 7:
             outs[2].start()
 
-    def wide(row):
-        return jnp.concatenate([row] * (HALF // 128), axis=1)
-
     def placed(block, row):
-        second = wide(row)
+        second = jnp.concatenate([row] * (block.shape[1] // 128), axis=1)
         block = block.astype(F32)
-        return (block * (1.0 - second), block * second)
-
-    def term(q, r, c):
-        return placed(cbuf[q * 8 + r, :, pl.ds(HALF * c, HALF)], row_of(q, r, me))
+        return [block * (1.0 - second), block * second]
+
+    def plus(left, right):
+        return [u + v for u, v in zip(left, right)]
+
+    def mine(q, r, cols):
+        return placed(cbuf[q * 8 + r, :, pl.ds(*cols)], row_of(q, r, me))
+
+    def ours(r, cols):
+        other = placed(cm[r, :, pl.ds(cols[0] - XW, cols[1])], row_of(0, r, mate))
+        return plus(mine(0, r, cols), other)
 
     def back_copy(q, way, hops, c):
-        return pltpu.make_async_remote_copy(
-            src_ref=sbuf.at[q, way, c] if hops == 2 else rbuf.at[q, way, 1, c],
-            dst_ref=rbuf.at[q, way, hops - 1, c],
+        cols = pl.ds(*XC[c])
+        return pltpu.make_async_remote_copy(
+            src_ref=sbuf.at[q, way, :, :, cols] if hops == 2 else rbuf.at[q, way, 1, :, :, cols],
+            dst_ref=rbuf.at[q, way, hops - 1, :, :, cols],
             send_sem=rs_send.at[q, way, hops - 1, c],
             recv_sem=rs_recv.at[q, way, hops - 1, c],
             device_id=(n, ring[way]),
@@ -393,79 +424,126 @@
 
     def back_send(q, way, hops, c):
         r = slot(hops, 1 - way)
-        if hops == 4:
-            if q == 1:
-                raw_copy(q, way, 2).start()
-            return
-        if hops == 3:
-            if c == way:
-                raw_copy(q, way, 2).wait_recv()
-                raw_copy(q, way, 3).start()
-            if q == 1:
-                raw_copy(q, way, c).start()
-            return
-        sums = term(q, r, c)
+        cols = pl.ds(*XC[c])
+        sums = mine(q, r, XC[c])
         if hops == 2:
             raw_copy(q, way, c).wait_recv()
-            more = placed(raw[q, way, c], row_of(q, r, ring[1 - way]))
-            sums = [u + v for u, v in zip(sums, more)]
+            sums = plus(sums, placed(raw[q, way, :, cols], row_of(q, r, ring[1 - way])))
             if c == way:
                 raw_copy(q, way, 3).wait_recv()
-                more = placed(far[q, way], row_of(q, r, beyond[1 - way]))
-                sums = [u + v for u, v in zip(sums, more)]
+                sums = plus(sums, placed(far[q, way, :, cols], row_of(q, r, beyond[1 - way])))
             for b in range(2):
-                sbuf[q, way, c, b] = sums[b].astype(BF)
+                sbuf[q, way, b, :, cols] = sums[b].astype(BF)
         else:
             back_copy(q, way, 2, c).wait_recv()
             for b in range(2):
-                rbuf[q, way, 1, c, b] = (rbuf[q, way, 1, c, b].astype(F32) + sums[b]).astype(BF)
+                rbuf[q, way, 1, b, :, cols] = (
+                    rbuf[q, way, 1, b, :, cols].astype(F32) + sums[b]
+                ).astype(BF)
         back_copy(q, way, hops, c).start()
 
-    steps = [
-        (q, hops, turn)
-        for q in (1, 0)
-        for hops in (4, 3, 2, 1)
-        for turn in range(2)
-        if hops < 4 or turn == 0
-    ]
-
-    def z_copy(c):
-        return pltpu.make_async_remote_copy(
-            src_ref=zsend.at[c],
-            dst_ref=zrecv.at[c],
-            send_sem=z_send.at[c],
-            recv_sem=z_recv.at[c],
-            device_id=(n, mate),
-            device_id_type=MESH,
-        )
-
     def total(q, c):
-        parts = term(q, 0, c)
+        cols = pl.ds(*XC[c])
+        sums = mine(q, 0, XC[c])
         for way in range(2):
             back_copy(q, way, 1, c).wait_recv()
-        return [
-            parts[b] + rbuf[q, 0, 0, c, b].astype(F32) + rbuf[q, 1, 0, c, b].astype(F32)
-            for b in range(2)
-        ]
-
-    for i, (q, hops, turn) in enumerate(steps):
+            sums = plus(sums, [rbuf[q, way, 0, b, :, cols].astype(F32) for b in range(2)])
+        return sums
+
+    def joint_copy(way, hops, c):
+        cols = pl.ds(ZC[c][0] - XW, ZC[c][1])
+        fresh = hops == 4 or (hops == 3 and c != way)
+        return pltpu.make_async_remote_copy(
+            src_ref=zst.at[way, 4 - hops, :, :, cols] if fresh else zr.at[way, hops, :, :, cols],
+            dst_ref=zr.at[way, hops - 1, :, :, cols],
+            send_sem=t_send.at[way, hops - 1, c],
+            recv_sem=t_recv.at[way, hops - 1, c],
+            device_id=(n, ring[way]),
+            device_id_type=MESH,
+        )
+
+    def joint_send(way, hops, c):
+        cols = pl.ds(ZC[c][0] - XW, ZC[c][1])
+        sums = ours(slot(hops, 1 - way), ZC[c])
+        if hops == 4 or (hops == 3 and c != way):
+            for b in range(2):
+                zst[way, 4 - hops, b, :, cols] = sums[b].astype(BF)
+        else:
+            joint_copy(way, hops + 1, c).wait_recv()
+            for b in range(2):
+                zr[way, hops, b, :, cols] = (
+                    zr[way, hops, b, :, cols].astype(F32) + sums[b]
+                ).astype(BF)
+        joint_copy(way, hops, c).start()
+
+    def z_copy(c, leg):
+        cols = pl.ds(*XC[c])
+        return pltpu.make_async_remote_copy(
+            src_ref=zl.at[:, :, cols] if leg else zsend.at[:, :, cols],
+            dst_ref=zrecv.at[:, :, cols] if leg else zl.at[:, :, cols],
+            send_sem=z_send.at[c, leg],
+            recv_sem=z_recv.at[c, leg],
+            device_id=(lax.rem(n + NODES // 2, NODES), zside[c]),
+            device_id_type=MESH,
+        )
+
+    for way in range(2):
+        for k in (2, 0, 1):
+            raw_copy(1, way, k).start()
+    for r in range(6, 8):
+        across(r, 0).start()
+    grad_piece(0)
+    hand_across(0, 4)
+    for q in (1, 0):
         for way in range(2):
-            back_send(q, way, hops, way ^ turn)
-        if i < 8:
-            grad_piece(i)
-        if i == 7:
-            for c in range(2):
-                sums = total(1, c)
-                for b in range(2):
-                    zsend[c, b] = sums[b].astype(BF)
-                z_copy(c).start()
+            raw_copy(q, way, 2).wait_recv()
+            raw_copy(q, way, 3).start()
+    grad_piece(1)
+    for i, (q, hops) in enumerate(((1, 2), (0, 2), (1, 1), (0, 1))):
+        for turn in range(2):
+            for way in range(2):
+                back_send(q, way, hops, way ^ turn)
+            if i < 3:
+                grad_piece(2 + 2 * i + turn)
+        if i == 0:
+            hand_across(4, 6)
+        if i == 1:
+            hand_across(6, 8)
+    for c in range(2):
+        sums = total(1, c)
+        for b in range(2):
+            zsend[b, :, pl.ds(*XC[c])] = sums[b].astype(BF)
+        z_copy(c, 0).start()
+    for r in (7, 5, 6, 3, 4, 1, 2, 0):
+        across(r, 1).wait_recv()
+        if r == 7:
+            for way in range(2):
+                joint_send(way, 4, way)
+    for turn in range(2):
+        for way in range(2):
+            joint_send(way, 3, way ^ 1 ^ turn)
+    for c in range(2):
+        z_copy(c, 0).wait_recv()
+        z_copy(c, 1).start()
+    for hops in (2, 1):
+        for turn in range(2):
+            for way in range(2):
+                joint_send(way, hops, way ^ 1 ^ turn)
     for c in range(2):
         sums = total(0, c)
-        z_copy(c).wait_recv()
+        z_copy(c, 1).wait_recv()
         for b in range(2):
-            dt_v[pl.ds(BLK * b, BLK), pl.ds(HALF * c, HALF)] = (
-                sums[b] + zrecv[c, b].astype(F32)
+            dt_v[pl.ds(BLK * b, BLK), pl.ds(*XC[c])] = (
+                sums[b] + zrecv[b, :, pl.ds(*XC[c])].astype(F32)
             ).astype(BF)
+    for c in (1, 0):
+        cols = pl.ds(ZC[c][0] - XW, ZC[c][1])
+        sums = ours(0, ZC[c])
+        for way in range(2):
+            joint_copy(way, 1, c).wait_recv()
+            sums = plus(sums, [zr[way, 0, b, :, cols].astype(F32) for b in range(2)])
+        for b in range(2):
+            dt_v[pl.ds(BLK * b, BLK), pl.ds(*ZC[c])] = sums[b].astype(BF)
     outs[3].start()
 
     for q in range(2):
@@ -489,7 +567,16 @@
     each_peer(lambda k: spread(k).wait_send())
     each_peer(lambda k: collect(k).wait_send())
     for c in range(2):
-        z_copy(c).wait_send()
+        for leg in range(2):
+            z_copy(c, leg).wait_send()
+    for r in range(8):
+        for leg in range(2):
+            across(r, leg).wait_send()
+    for way in range(2):
+        joint_copy(way, 4, way).wait_send()
+        for hops in (3, 2, 1):
+            for c in range(2):
+                joint_copy(way, hops, c).wait_send()
     for c in outs:
         c.wait()
 
@@ -499,9 +586,8 @@
     live = jnp.arange(2, dtype=jnp.int32) < counts[0]
     gates = router_gate.T.reshape(4, 2, 1, BLK)
     hot = (routes[0].T[:, :, None] == groups) & live[None, :, None]
-    weights = jnp.sum(jnp.where(hot[:, :, :, None], gates, 0.0), axis=(0, 1))
-    second = jnp.any(routes[0, 1][:, None] == groups, axis=0).astype(F32)
-    meta = jnp.concatenate([weights, jnp.broadcast_to(second[:, None], (GROUP, BLK))], axis=0)
+    signed = gates * jnp.array([1.0, -1.0], F32)[None, :, None, None]
+    meta = jnp.sum(jnp.where(hot[:, :, :, None], signed, 0.0), axis=(0, 1))
 
     any_ = pl.BlockSpec(memory_space=pl.ANY)
     dma = pltpu.SemaphoreType.DMA
@@ -514,7 +600,7 @@
         in_specs=[pl.BlockSpec(memory_space=pltpu.SMEM)] + [any_] * 6,
         out_specs=[any_] * 4,
         scratch_shapes=[
-            pltpu.VMEM((2, 8, 32, 128), F32),
+            pltpu.VMEM((2, 8, GROUP, BLK), F32),
             pltpu.VMEM((2, 5, 2 * BLK, D), BF),
             pltpu.VMEM((2, 5, 2 * BLK, D), BF),
             pltpu.VMEM((16, BLK, D), BF),
@@ -525,14 +611,19 @@
             pltpu.VMEM((2, 2, 3, BLK, D), BF),
             pltpu.VMEM((2, 2, BLK, D), BF),
             pltpu.VMEM((2, 2 * BLK, D), BF),
-            pltpu.VMEM((2, 2, 2, BLK, HALF), BF),
-            pltpu.VMEM((2, 2, BLK, HALF), BF),
-            pltpu.VMEM((2, 2, BLK, HALF), BF),
-            pltpu.VMEM((2, 2, 2, 2, BLK, HALF), BF),
-            pltpu.VMEM((2, 2, 2, 2, 2, BLK, HALF), BF),
-            pltpu.VMEM((2, 2, BLK, HALF), BF),
-            pltpu.VMEM((2, 2, BLK, HALF), BF),
-            pltpu.VMEM((32, 128), F32),
+            pltpu.VMEM((GROUP, BLK), F32),
+            pltpu.VMEM((2, 2, BLK, XW), BF),
+            pltpu.VMEM((2, 2, BLK, XW), BF),
+            pltpu.VMEM((2, 2, BLK, XW), BF),
+            pltpu.VMEM((2, 2, 2, BLK, XW), BF),
+            pltpu.VMEM((2, 2, 2, 2, BLK, XW), BF),
+            pltpu.VMEM((2, 2, 2, BLK, D - XW), BF),
+            pltpu.VMEM((2, 4, 2, BLK, D - XW), BF),
+            pltpu.VMEM((8, BLK, D - XW), BF),
+            pltpu.VMEM((8, BLK, D - XW), BF),
+            pltpu.VMEM((2, BLK, XW), BF),
+            pltpu.VMEM((2, BLK, XW), BF),
+            pltpu.VMEM((2, BLK, XW), BF),
             pltpu.VMEM((16, 2, PART, H), BF),
             pltpu.VMEM((NODES, PART, H), BF),
             pltpu.VMEM((NODES, PART, H), BF),
@@ -543,7 +634,8 @@
             pltpu.VMEM((2 * BLK, D), BF),
             dma((2, 2, 4, 3)), dma((2, 2, 4, 3)), dma((2, 2, 4)), dma((2, 2, 4)), dma((3, 2)), dma((3, 2)),
             dma((NODES,)), dma((NODES,)), dma((NODES,)), dma((NODES,)),
-            dma((2, 2, 4)), dma((2, 2, 4)), dma((2, 2, 2, 2)), dma((2, 2, 2, 2)), dma((2,)), dma((2,)), dma((9,)), dma((4,)),
+            dma((2, 2, 4)), dma((2, 2, 4)), dma((2, 2, 2, 2)), dma((2, 2, 2, 2)), dma((2, 4, 2)), dma((2, 4, 2)),
+            dma((8, 2)), dma((8, 2)), dma((2, 2)), dma((2, 2)), dma((9,)), dma((4,)),
         ],
         compiler_params=pltpu.CompilerParams(
             collective_id=0, has_side_effects=True, vmem_limit_bytes=67043328

time: 253 us -> 232 us (0.917)
  the two profiles are of different devices: /device:TPU:70 before, /device:TPU:6 now
where the time goes in v3:
time: 232 us; the launch traced here: 230 us
  Pallas kernels  220 us (95%)
  local copies, waits for them, and re-layouts  7.12 us (3%)
    pallas_call x1, Pallas kernels, on_device(): pl.pallas_call(kernel, out_shape=(shape((2 * BLK, D), BF), shape((D, H),...  220 us
    unnamed x16, local copies, waits for them, and re-layouts  7.01 us

profile of v3, /device:TPU:6, one launch (start us, length us, event | category | flops | bytes accessed | tf_op | source)
XLA Modules:
  0.0 229.6 jit_solution(15496909978669971068)
XLA Ops:
  1.3 0.0 copy-start.4
  1.3 0.7 copy-done.4
  2.0 0.0 copy-start.3
  2.0 0.1 copy.15
  2.1 0.1 compare_and_fusion
  2.1 0.5 copy-done.3
  2.7 0.0 copy-start.5
  2.7 0.6 copy-done.5
  3.3 0.1 broadcast_multiply_fusion
  3.4 0.7 select_reduce_fusion.meta_in
  4.1 220.3 %moe_step.1 = (bf16[256,1024]{1,0:T(8,128)(2,1)}, bf16[1024,256]{1,0:T(8,128)(2,1)}, bf16[1024,256]{1,0:T(8,128)(2,1)}, bf16[256,1024]{1,0:T(8,128)(2,1)}) custom-call(s32[32]{0:T(128)} %partner.1, f32[16,128]{1,0:T(8,128)} %select_reduce_fusion.meta_in, bf16[256,1024]{1,0:T(8,128)(2,1)} %tok_in.1, bf16[256,1024]{1,0:T(8,128)(2,1)} %gr_in.1, ...), custom_call_target="tpu_custom_call" | custom-call | tf_op jit(solution)/shard_map/moe_step/pallas_call | solution.py:595
  224.4 0.0 copy-start.2
  224.4 1.9 copy.21
  226.3 0.0 copy-done.2
  226.3 0.0 copy-start.1
  226.3 0.8 copy.22
  227.1 0.4 copy-done.1
  227.6 0.0 copy-start
  227.6 0.8 copy.23
  228.4 0.4 copy-done
  228.8 0.8 copy.24
  (2 shorter events, 0.0 us)
Async XLA Ops:
  1.3 0.7 copy-start.4
  2.0 0.7 copy-start.3
  2.7 0.7 copy-start.5
  224.4 1.9 copy-start.2
  226.3 1.2 copy-start.1
  227.6 1.2 copy-start

commit v4 on v3

--- a/solution.py
+++ b/solution.py
@@ -16,9 +16,9 @@
 BLK = 128
 D = 1024
 H = 256
-XW = 640
-XC = ((0, 384), (384, 256))
-ZC = ((640, 256), (896, 128))
+XW = 768
+XC = ((0, 384), (384, 384))
+ZC = ((768, 128), (896, 128))
 PART = 96
 
 
@@ -37,9 +37,9 @@
 
 
 def kernel(
-    partner, meta_in, tok_in, gr_in, wg_in, wu_in, wd_in,
+    partner, routes, counts, gates_in, tok_in, gr_in, wg_in, wu_in, wd_in,
     dt_out, dg_out, du_out, dd_out,
-    meta, tok, gr, xs, gs, gact, hact, cbuf, cut, relay, zrel, zmeta,
+    gates, meta, tok, gr, xs, gs, gact, hact, cbuf, cut, relay, zrel, zmeta,
     raw, near, far, sbuf, rbuf, zst, zr, zf, cm, zsend, zl, zrecv,
     pack, mixed, stage, wrec, dg_v, du_v, dd_v, dt_v,
     g_send, g_recv, s_send, s_recv, m_send, m_recv, wa_send, wa_recv, wb_send, wb_recv,
@@ -68,11 +68,11 @@
             )
         )
     owns = [
-        pltpu.make_async_copy(meta_in, meta.at[0, 0], loc.at[6]),
+        pltpu.make_async_copy(gates_in, gates, loc.at[6]),
         pltpu.make_async_copy(tok_in, tok.at[0, 0], loc.at[7]),
         pltpu.make_async_copy(gr_in, gr.at[0, 0], loc.at[8]),
     ]
-    for c in locals_ + owns:
+    for c in owns + locals_:
         c.start()
 
     barrier = pltpu.get_barrier_semaphore()
@@ -89,10 +89,20 @@
     pl.semaphore_signal(
         barrier, inc=1, device_id=(lax.rem(n + NODES // 2, NODES), mate), device_id_type=MESH
     )
+
+    owns[0].wait()
+    device = lax.broadcasted_iota(jnp.int32, (GROUP, BLK), 0)
+    table = jnp.zeros((GROUP, BLK), F32)
+    for b in range(2):
+        for k in range(4):
+            asked = jnp.where(b < counts[0], routes[b, k], -1)
+            weights = gates[pl.ds(k, 1), pl.ds(BLK * b, BLK)]
+            table = jnp.where(device == asked, -weights if b else weights, table)
+    meta[0, 0] = table
     pl.semaphore_wait(barrier, NODES - 1 + 3)
 
     bufs = (meta, tok, gr)
-    ins = (meta_in, tok_in, gr_in)
+    ins = (meta.at[0, 0], tok_in, gr_in)
 
     def gather(q, way, hops, c):
         src = ins[c] if q == 0 and hops == 1 else bufs[c].at[q, slot(hops - 1, way)]
@@ -310,7 +320,7 @@
     for c in locals_:
         c.wait()
     mixed[n] = pack[n // 2, lax.rem(n, 2)]
-    for c in owns:
+    for c in owns[1:]:
         c.wait()
     pick(0, 0, 1)
     for c in range(2):
@@ -499,36 +509,52 @@
             raw_copy(q, way, 2).wait_recv()
             raw_copy(q, way, 3).start()
     grad_piece(1)
-    for i, (q, hops) in enumerate(((1, 2), (0, 2), (1, 1), (0, 1))):
+    def ring_step(q, hops, turn):
+        for way in range(2):
+            back_send(q, way, hops, way ^ turn)
+
+    def joint_step(hops):
         for turn in range(2):
             for way in range(2):
-                back_send(q, way, hops, way ^ turn)
-            if i < 3:
-                grad_piece(2 + 2 * i + turn)
-        if i == 0:
-            hand_across(4, 6)
-        if i == 1:
-            hand_across(6, 8)
+                joint_send(way, hops, way ^ 1 ^ turn)
+
+    ring_step(1, 2, 0)
+    grad_piece(2)
+    ring_step(1, 2, 1)
+    hand_across(4, 6)
+    ring_step(0, 2, 0)
+    grad_piece(3)
+    hand_across(6, 8)
+    ring_step(1, 1, 0)
+    grad_piece(4)
+    ring_step(1, 1, 1)
     for c in range(2):
         sums = total(1, c)
         for b in range(2):
             zsend[b, :, pl.ds(*XC[c])] = sums[b].astype(BF)
         z_copy(c, 0).start()
-    for r in (7, 5, 6, 3, 4, 1, 2, 0):
+    ring_step(0, 2, 1)
+    grad_piece(5)
+    across(7, 1).wait_recv()
+    for way in range(2):
+        joint_send(way, 4, way)
+    ring_step(0, 1, 0)
+    grad_piece(6)
+    for r in (5, 6):
         across(r, 1).wait_recv()
-        if r == 7:
-            for way in range(2):
-                joint_send(way, 4, way)
-    for turn in range(2):
-        for way in range(2):
-            joint_send(way, 3, way ^ 1 ^ turn)
+    joint_step(3)
     for c in range(2):
         z_copy(c, 0).wait_recv()
         z_copy(c, 1).start()
-    for hops in (2, 1):
-        for turn in range(2):
-            for way in range(2):
-                joint_send(way, hops, way ^ 1 ^ turn)
+    ring_step(0, 1, 1)
+    for r in (3, 4):
+        across(r, 1).wait_recv()
+    joint_step(2)
+    for r in (1, 2):
+        across(r, 1).wait_recv()
+    joint_step(1)
+    grad_piece(7)
+    across(0, 1).wait_recv()
     for c in range(2):
         sums = total(0, c)
         z_copy(c, 1).wait_recv()
@@ -581,14 +607,27 @@
         c.wait()
 
 
+def hand_out(a, b, c, d, w, x, y, z, va, vb, vc, vd, into, out):
+    triples = ((a, va, w), (b, vb, x), (c, vc, y), (d, vd, z))
+    parts = []
+    for i, (src, mid, dst) in enumerate(triples):
+        rows = src.shape[0] // 2
+        for j in range(2):
+            at = pl.ds(rows * j, rows)
+            parts.append((
+                pltpu.make_async_copy(src.at[at], mid.at[at], into.at[2 * i + j]),
+                pltpu.make_async_copy(mid.at[at], dst.at[at], out.at[2 * i + j]),
+            ))
+    for first, second in parts:
+        first.start()
+    for first, second in parts:
+        first.wait()
+        second.start()
+    for first, second in parts:
+        second.wait()
+
+
 def on_device(tokens, grad_out, router_gate, counts, routes, partner, w_gate, w_up, w_down):
-    groups = jnp.arange(GROUP, dtype=jnp.int32)
-    live = jnp.arange(2, dtype=jnp.int32) < counts[0]
-    gates = router_gate.T.reshape(4, 2, 1, BLK)
-    hot = (routes[0].T[:, :, None] == groups) & live[None, :, None]
-    signed = gates * jnp.array([1.0, -1.0], F32)[None, :, None, None]
-    meta = jnp.sum(jnp.where(hot[:, :, :, None], signed, 0.0), axis=(0, 1))
-
     any_ = pl.BlockSpec(memory_space=pl.ANY)
     dma = pltpu.SemaphoreType.DMA
     shape = jax.ShapeDtypeStruct
@@ -597,9 +636,10 @@
         out_shape=(
             shape((2 * BLK, D), BF), shape((D, H), BF), shape((D, H), BF), shape((H, D), BF),
         ),
-        in_specs=[pl.BlockSpec(memory_space=pltpu.SMEM)] + [any_] * 6,
+        in_specs=[pl.BlockSpec(memory_space=pltpu.SMEM)] * 3 + [any_] * 6,
         out_specs=[any_] * 4,
         scratch_shapes=[
+            pltpu.VMEM((4, 2 * BLK), F32),
             pltpu.VMEM((2, 8, GROUP, BLK), F32),
             pltpu.VMEM((2, 5, 2 * BLK, D), BF),
             pltpu.VMEM((2, 5, 2 * BLK, D), BF),
@@ -642,10 +682,17 @@
         ),
         name="moe_step",
     )(
-        partner, meta, tokens, grad_out,
+        partner, routes.reshape(2, 4), counts, router_gate.T, tokens, grad_out,
         w_gate.reshape(16, 2, 32, H), w_up.reshape(16, 2, 32, H), w_down.reshape(16, 16, D),
     )
-    dt, dg, du, dd = outs
+    dt, dg, du, dd = pl.pallas_call(
+        hand_out,
+        out_shape=tuple(shape(o.shape, BF) for o in outs),
+        in_specs=[any_] * 4,
+        out_specs=[any_] * 4,
+        scratch_shapes=[pltpu.VMEM(o.shape, BF) for o in outs] + [dma((8,)), dma((8,))],
+        name="hand_out",
+    )(*outs)
     return dt, dg.reshape(1, D, H), du.reshape(1, D, H), dd.reshape(1, H, D)
 
 

time: 232 us -> 224 us (0.966)
  local copies, waits for them, and re-layouts: 7.12 us -> 0 us
    unnamed x16 -> x0, local copies, waits for them, and re-layouts: 7.01 us -> none
    pallas_call x0 -> x1, Pallas kernels: none -> 2.4 us  [on_device(): pl.pallas_call(hand_out, out_shape=tuple((shape(o.shape, BF) for o in out...]
where the time goes in v4:
time: 224 us; the launch traced here: 222 us
  Pallas kernels  221 us (99%)
    pallas_call x1, Pallas kernels, on_device(): pl.pallas_call(kernel, out_shape=(shape((2 * BLK, D), BF), shape((D, H),...  219 us

profile of v4, /device:TPU:6, one launch (start us, length us, event | category | flops | bytes accessed | tf_op | source)
XLA Modules:
  0.0 222.5 jit_solution(9043795752792580555)
XLA Ops:
  1.3 218.6 %moe_step.1 = (bf16[256,1024]{1,0:T(8,128)(2,1)}, bf16[1024,256]{1,0:T(8,128)(2,1)}, bf16[1024,256]{1,0:T(8,128)(2,1)}, bf16[256,1024]{1,0:T(8,128)(2,1)}) custom-call(s32[32]{0:T(128)} %partner.1, s32[2,4]{1,0:T(2,128)} %bitcast.12, s32[1]{0:T(128)S(6)} %copy.13.counts, f32[4,256]{1,0:T(4,128)} %bitcast.11, bf16[256,1024]{1,0:T(8,128)(2,1)} %tok_in.1, ...), custom_call_target="tpu_custom_call" | custom-call | tf_op jit(solution)/shard_map/moe_step/pallas_call | solution.py:634
  219.9 2.4 %hand_out.1 = (bf16[256,1024]{1,0:T(8,128)(2,1)}, bf16[1024,256]{1,0:T(8,128)(2,1)}, bf16[1024,256]{1,0:T(8,128)(2,1)}, bf16[256,1024]{1,0:T(8,128)(2,1)}) custom-call(bf16[256,1024]{1,0:T(8,128)(2,1)} %get-tuple-element.12.a, bf16[1024,256]{1,0:T(8,128)(2,1)} %get-tuple-element.13.b, bf16[1024,256]{1,0:T(8,128)(2,1)} %get-tuple-element.14.c, ...), custom_call_target="tpu_custom_call" | custom-call | tf_op jit(solution)/shard_map/hand_out/pallas_call | solution.py:688

commit v5 on v4

--- a/solution.py
+++ b/solution.py
@@ -16,9 +16,9 @@
 BLK = 128
 D = 1024
 H = 256
-XW = 768
-XC = ((0, 384), (384, 384))
-ZC = ((768, 128), (896, 128))
+XW = 640
+XC = ((0, 384), (384, 256))
+ZC = ((640, 256), (896, 128))
 PART = 96
 
 
@@ -365,20 +365,21 @@
         arrive(1, 2, c)
     pick(1, 3, 5)
     each_peer(lambda k: collect(k).wait_recv())
+    run(4, 6)
+    for r in range(4):
+        across(r, 0).start()
+    for c in range(2):
+        arrive(1, 3, c)
     run(0, 2)
-    for c in range(2):
-        arrive(1, 3, c)
+    arrive(1, 3, 2)
     run(2, 4)
-    arrive(1, 3, 2)
     for way in range(2):
         for k in (2, 0, 1):
             raw_copy(0, way, k).start()
-    run(4, 6)
-    for r in range(4):
-        across(r, 0).start()
     run(6, 7)
     for r in range(4, 6):
         across(r, 0).start()
+    hand_across(0, 4)
     for c in range(3):
         arrive(1, 4, c)
     run(7, 8)
@@ -503,7 +504,6 @@
     for r in range(6, 8):
         across(r, 0).start()
     grad_piece(0)
-    hand_across(0, 4)
     for q in (1, 0):
         for way in range(2):
             raw_copy(q, way, 2).wait_recv()

time: 224 us -> 221 us (0.987)
  no operation moved by 1% of the time
where the time goes in v5:
time: 221 us
  Pallas kernels  220 us (100%)
    pallas_call x1, Pallas kernels, on_device(): pl.pallas_call(kernel, out_shape=(shape((2 * BLK, D), BF), shape((D, H),...  217 us

profile of v5, /device:TPU:6, one launch (start us, length us, event | category | flops | bytes accessed | tf_op | source)
XLA Modules:
  0.0 221.0 jit_solution(9592741941232439278)
XLA Ops:
  1.3 217.2 %moe_step.1 = (bf16[256,1024]{1,0:T(8,128)(2,1)}, bf16[1024,256]{1,0:T(8,128)(2,1)}, bf16[1024,256]{1,0:T(8,128)(2,1)}, bf16[256,1024]{1,0:T(8,128)(2,1)}) custom-call(s32[32]{0:T(128)} %partner.1, s32[2,4]{1,0:T(2,128)} %bitcast.12, s32[1]{0:T(128)S(6)} %copy.13.counts, f32[4,256]{1,0:T(4,128)} %bitcast.11, bf16[256,1024]{1,0:T(8,128)(2,1)} %tok_in.1, ...), custom_call_target="tpu_custom_call" | custom-call | tf_op jit(solution)/shard_map/moe_step/pallas_call | solution.py:634
  218.5 2.4 %hand_out.1 = (bf16[256,1024]{1,0:T(8,128)(2,1)}, bf16[1024,256]{1,0:T(8,128)(2,1)}, bf16[1024,256]{1,0:T(8,128)(2,1)}, bf16[256,1024]{1,0:T(8,128)(2,1)}) custom-call(bf16[256,1024]{1,0:T(8,128)(2,1)} %get-tuple-element.12.a, bf16[1024,256]{1,0:T(8,128)(2,1)} %get-tuple-element.13.b, bf16[1024,256]{1,0:T(8,128)(2,1)} %get-tuple-element.14.c, ...), custom_call_target="tpu_custom_call" | custom-call | tf_op jit(solution)/shard_map/hand_out/pallas_call | solution.py:688

commit v6 on v5

--- a/solution.py
+++ b/solution.py
@@ -463,7 +463,7 @@
 
     def joint_copy(way, hops, c):
         cols = pl.ds(ZC[c][0] - XW, ZC[c][1])
-        fresh = hops == 4 or (hops == 3 and c != way)
+        fresh = hops == 4 or (hops == 3 and c == way)
         return pltpu.make_async_remote_copy(
             src_ref=zst.at[way, 4 - hops, :, :, cols] if fresh else zr.at[way, hops, :, :, cols],
             dst_ref=zr.at[way, hops - 1, :, :, cols],
@@ -476,7 +476,7 @@
     def joint_send(way, hops, c):
         cols = pl.ds(ZC[c][0] - XW, ZC[c][1])
         sums = ours(slot(hops, 1 - way), ZC[c])
-        if hops == 4 or (hops == 3 and c != way):
+        if hops == 4 or (hops == 3 and c == way):
             for b in range(2):
                 zst[way, 4 - hops, b, :, cols] = sums[b].astype(BF)
         else:
@@ -516,7 +516,7 @@
     def joint_step(hops):
         for turn in range(2):
             for way in range(2):
-                joint_send(way, hops, way ^ 1 ^ turn)
+                joint_send(way, hops, way ^ turn)
 
     ring_step(1, 2, 0)
     grad_piece(2)
@@ -537,7 +537,7 @@
     grad_piece(5)
     across(7, 1).wait_recv()
     for way in range(2):
-        joint_send(way, 4, way)
+        joint_send(way, 4, 1 - way)
     ring_step(0, 1, 0)
     grad_piece(6)
     for r in (5, 6):
@@ -599,7 +599,7 @@
         for leg in range(2):
             across(r, leg).wait_send()
     for way in range(2):
-        joint_copy(way, 4, way).wait_send()
+        joint_copy(way, 4, 1 - way).wait_send()
         for hops in (3, 2, 1):
             for c in range(2):
                 joint_copy(way, hops, c).wait_send()

time: 221 us -> 222 us (level)
  no operation moved by 1% of the time
where the time goes in v6:
time: 222 us; the launch traced here: 220 us
  Pallas kernels  219 us (99%)
    pallas_call x1, Pallas kernels, on_device(): pl.pallas_call(kernel, out_shape=(shape((2 * BLK, D), BF), shape((D, H),...  217 us

profile of v6, /device:TPU:6, one launch (start us, length us, event | category | flops | bytes accessed | tf_op | source)
XLA Modules:
  0.0 220.3 jit_solution(16945903410393879017)
XLA Ops:
  1.3 216.5 %moe_step.1 = (bf16[256,1024]{1,0:T(8,128)(2,1)}, bf16[1024,256]{1,0:T(8,128)(2,1)}, bf16[1024,256]{1,0:T(8,128)(2,1)}, bf16[256,1024]{1,0:T(8,128)(2,1)}) custom-call(s32[32]{0:T(128)} %partner.1, s32[2,4]{1,0:T(2,128)} %bitcast.12, s32[1]{0:T(128)S(6)} %copy.13.counts, f32[4,256]{1,0:T(4,128)} %bitcast.11, bf16[256,1024]{1,0:T(8,128)(2,1)} %tok_in.1, ...), custom_call_target="tpu_custom_call" | custom-call | tf_op jit(solution)/shard_map/moe_step/pallas_call | solution.py:634
  217.8 2.4 %hand_out.1 = (bf16[256,1024]{1,0:T(8,128)(2,1)}, bf16[1024,256]{1,0:T(8,128)(2,1)}, bf16[1024,256]{1,0:T(8,128)(2,1)}, bf16[256,1024]{1,0:T(8,128)(2,1)}) custom-call(bf16[256,1024]{1,0:T(8,128)(2,1)} %get-tuple-element.12.a, bf16[1024,256]{1,0:T(8,128)(2,1)} %get-tuple-element.13.b, bf16[1024,256]{1,0:T(8,128)(2,1)} %get-tuple-element.14.c, ...), custom_call_target="tpu_custom_call" | custom-call | tf_op jit(solution)/shard_map/hand_out/pallas_call | solution.py:688
